TPU v7x, 32 devices: a whole 2x2x4 slice. The times are simulated.
32 devices in a mesh: seq: 4 (over z), fsdp: 8 (over y, x, core).
Axes of the slice: x: 2, y: 2, z: 4, core: 2. Of those that a mesh axis runs over, the one named last changes fastest.
Arguments:
- block_input: bfloat16 [4096, 1024], P(('seq', 'fsdp')), may hold values from -6 to 6
- out_grad: bfloat16 [4096, 1024], P(('seq', 'fsdp')), may hold values from -6 to 6
- attn_gain: bfloat16 [1024], P('fsdp'), may hold values from 0.5 to 1.5
- attn_shift: bfloat16 [1024], P('fsdp'), may hold values from -1.75 to 1.75
- qkv_weight: bfloat16 [1024, 3072], P('fsdp'), may hold values from -0.1875 to 0.1875
- query_bias: bfloat16 [1024], P('fsdp'), may hold values from -3 to 3
- value_bias: bfloat16 [1024], P('fsdp'), may hold values from -0.625 to 0.625
- out_weight: bfloat16 [1024, 1024], P('fsdp'), may hold values from -1.5 to 1.5
- out_bias: bfloat16 [1024], P('fsdp'), may hold values from -1.75 to 1.75
- mlp_gain: bfloat16 [1024], P('fsdp'), may hold values from 0.5 to 1.5
- mlp_shift: bfloat16 [1024], P('fsdp'), may hold values from -1.75 to 1.75
- fc_weight: bfloat16 [1024, 4096], P(None, 'fsdp'), may hold values from -0.1875 to 0.1875
- fc_bias: bfloat16 [4096], P('fsdp'), may hold values from -3 to 3
- proj_weight: bfloat16 [4096, 1024], P('fsdp'), may hold values from -0.09375 to 0.09375
- proj_bias: bfloat16 [1024], P('fsdp'), may hold values from -1.75 to 1.75
Outputs:
- block_output: bfloat16 [4096, 1024], P(('seq', 'fsdp'))
- input_grad: float32 [4096, 1024], P(('seq', 'fsdp'))
- grad_attn_gain: float32 [1024], P('fsdp')
- grad_attn_shift: float32 [1024], P('fsdp')
- grad_qkv_weight: float32 [1024, 3072], P('fsdp')
- grad_query_bias: float32 [1024], P('fsdp')
- grad_value_bias: float32 [1024], P('fsdp')
- grad_out_weight: float32 [1024, 1024], P('fsdp')
- grad_out_bias: float32 [1024], P('fsdp')
- grad_mlp_gain: float32 [1024], P('fsdp')
- grad_mlp_shift: float32 [1024], P('fsdp')
- grad_fc_weight: float32 [1024, 4096], P(None, 'fsdp')
- grad_fc_bias: float32 [4096], P('fsdp')
- grad_proj_weight: float32 [4096, 1024], P('fsdp')
- grad_proj_bias: float32 [1024], P('fsdp')
All inputs are finite; a program needn't handle non-finite values.
Results may differ from a plain program's by a relative error of at most 0.02.
Values may be sent and summed in bfloat16 or wider, within the bound.
A program may use at most 192 MiB of HBM per device.

v0:
```python
import math

import jax
import jax.numpy as jnp
from jax import lax
from jax.sharding import PartitionSpec as P

HEADS = 16


norm_eps = 1e-05
gelu_coef = 0.7978845608028654
cubic_coef = 0.044715


def norm_forward(values, gain_vec, shift_vec):
    centre = jnp.mean(values, axis=-1, keepdims=True)
    centred = values - centre
    inv_scale = lax.rsqrt(jnp.mean(centred * centred, axis=-1, keepdims=True) + norm_eps)
    normed = centred * inv_scale
    return (normed, inv_scale, normed * gain_vec + shift_vec)


def norm_backward(upstream, normed, inv_scale, gain_vec):
    scaled = upstream * gain_vec
    return inv_scale * (
        scaled
        - jnp.mean(scaled, axis=-1, keepdims=True)
        - normed * jnp.mean(scaled * normed, axis=-1, keepdims=True)
    )


def gelu_value(pre_act):
    return (
        0.5
        * pre_act
        * (1.0 + jnp.tanh(gelu_coef * (pre_act + cubic_coef * pre_act * pre_act * pre_act)))
    )


def gelu_slope(pre_act):
    tanh_val = jnp.tanh(gelu_coef * (pre_act + cubic_coef * pre_act * pre_act * pre_act))
    return 0.5 * (1.0 + tanh_val) + 0.5 * pre_act * (1.0 - tanh_val * tanh_val) * gelu_coef * (
        1.0 + 3.0 * cubic_coef * pre_act * pre_act
    )


def on_device(
    block_input,
    out_grad,
    attn_gain,
    attn_shift,
    qkv_weight,
    query_bias,
    value_bias,
    out_weight,
    out_bias,
    mlp_gain,
    mlp_shift,
    fc_weight,
    fc_bias,
    proj_weight,
    proj_bias,
):
    tok_local = block_input.shape[0]
    width = block_input.shape[1]
    groups = lax.axis_size("seq")
    shards = lax.axis_size("fsdp")
    shard_pos = lax.axis_index("fsdp")
    heads_group = HEADS // groups
    head_size = width // HEADS
    group_width = width // groups
    piece_len = shards * tok_local
    pair_count = groups // 2
    score_scale = 1.0 / math.sqrt(head_size)
    gathered = (
        lax.all_gather(attn_gain, "fsdp", axis=0, tiled=True),
        lax.all_gather(attn_shift, "fsdp", axis=0, tiled=True),
        lax.all_gather(qkv_weight, "fsdp", axis=0, tiled=True),
        lax.all_gather(query_bias, "fsdp", axis=0, tiled=True),
        lax.all_gather(value_bias, "fsdp", axis=0, tiled=True),
        lax.all_gather(out_weight, "fsdp", axis=0, tiled=True),
        lax.all_gather(out_bias, "fsdp", axis=0, tiled=True),
        lax.all_gather(mlp_gain, "fsdp", axis=0, tiled=True),
        lax.all_gather(mlp_shift, "fsdp", axis=0, tiled=True),
        lax.all_gather(fc_weight, "fsdp", axis=1, tiled=True),
        lax.all_gather(fc_bias, "fsdp", axis=0, tiled=True),
        lax.all_gather(proj_weight, "fsdp", axis=0, tiled=True),
        lax.all_gather(proj_bias, "fsdp", axis=0, tiled=True),
    )
    fc_full = gathered[9]
    fc_bias_full = gathered[10].astype(jnp.float32)
    proj_full = gathered[11]
    gain1 = gathered[0].astype(jnp.float32)
    shift1 = gathered[1].astype(jnp.float32)
    qkv_full = gathered[2]
    bias_row = jnp.concatenate(
        [
            gathered[3].astype(jnp.float32),
            jnp.zeros((width,), jnp.float32),
            gathered[4].astype(jnp.float32),
        ]
    )
    out_full = gathered[5]
    out_bias_full = gathered[6].astype(jnp.float32)
    gain2 = gathered[7].astype(jnp.float32)
    shift2 = gathered[8].astype(jnp.float32)
    proj_bias_full = gathered[-1].astype(jnp.float32)
    x_vals = block_input.astype(jnp.float32)
    normed1, rstd1, affine1 = norm_forward(x_vals, gain1, shift1)
    norm1_bf = affine1.astype(jnp.bfloat16)
    qkv_bf = (jnp.dot(norm1_bf, qkv_full, preferred_element_type=jnp.float32) + bias_row).astype(
        jnp.bfloat16
    )
    qkv_heads = lax.all_to_all(
        qkv_bf.reshape(1, tok_local, 3, groups, group_width),
        "seq",
        split_axis=3,
        concat_axis=0,
        tiled=True,
    )
    query_r = qkv_heads[:, :, 0, 0, :].reshape(groups, tok_local, heads_group, head_size)
    kv_own = qkv_heads[:, :, 1:3, 0, :].reshape(groups, 1, tok_local, 2, group_width)
    kv_all = lax.all_gather(kv_own, "fsdp", axis=1, tiled=True)
    kv_pieces = kv_all.reshape(groups, piece_len, 2, heads_group, head_size)
    row_pos = shard_pos * tok_local + jnp.arange(tok_local, dtype=jnp.int32)
    key_pos = jnp.arange(piece_len, dtype=jnp.int32)
    pair_rows = 2 * tok_local

    def query_positions(blk_idx):
        starts = (2 * blk_idx + jnp.arange(2, dtype=jnp.int32))[:, None] * piece_len
        return (starts + row_pos[None, :]).reshape(pair_rows)

    def forward_block(blk_idx, carry):
        out_acc, lse_acc = carry
        query_blk = lax.dynamic_slice_in_dim(query_r, 2 * blk_idx, 2, 0).reshape(
            pair_rows, heads_group, head_size
        )
        q_pos = query_positions(blk_idx)

        def forward_key_step(key_idx, inner):
            weighted, summed = inner
            kv_blk = lax.dynamic_index_in_dim(kv_pieces, key_idx, 0, keepdims=False)
            scores = (
                jnp.einsum(
                    "qhd,khd->hqk", query_blk, kv_blk[:, 0], preferred_element_type=jnp.float32
                )
                * score_scale
            )
            visible = (key_idx * piece_len + key_pos)[None, :] <= q_pos[:, None]
            weights = jnp.where(visible[None], jnp.exp(scores), 0.0)
            summed = summed + jnp.sum(weights, axis=-1)
            weighted = weighted + jnp.einsum(
                "hqk,khd->qhd",
                weights.astype(jnp.bfloat16),
                kv_blk[:, 1],
                preferred_element_type=jnp.float32,
            )
            return (weighted, summed)

        start_acc = (
            jnp.zeros((pair_rows, heads_group, head_size), jnp.float32),
            jnp.zeros((heads_group, pair_rows), jnp.float32),
        )
        weighted, summed = lax.fori_loop(0, 2 * blk_idx + 2, forward_key_step, start_acc)
        out_blk = (weighted / summed.T[:, :, None]).astype(jnp.bfloat16)
        out_acc = lax.dynamic_update_slice_in_dim(
            out_acc, out_blk.reshape(2, tok_local, group_width), 2 * blk_idx, 0
        )
        lse_acc = lax.dynamic_update_slice_in_dim(
            lse_acc, jnp.log(summed).T.reshape(2, tok_local, heads_group), 2 * blk_idx, 0
        )
        return (out_acc, lse_acc)

    out_heads, lse_heads = lax.fori_loop(
        0,
        pair_count,
        forward_block,
        (
            jnp.zeros((groups, tok_local, group_width), jnp.bfloat16),
            jnp.zeros((groups, tok_local, heads_group), jnp.float32),
        ),
    )
    attn_tok = lax.all_to_all(
        out_heads.reshape(groups, tok_local, 1, group_width),
        "seq",
        split_axis=0,
        concat_axis=2,
        tiled=True,
    ).reshape(tok_local, width)
    resid1 = (
        x_vals + jnp.dot(attn_tok, out_full, preferred_element_type=jnp.float32) + out_bias_full
    )
    normed2, rstd2, affine2 = norm_forward(resid1, gain2, shift2)
    norm2_bf = affine2.astype(jnp.bfloat16)
    grad_vals = out_grad.astype(jnp.float32)
    hidden_pre = jnp.dot(norm2_bf, fc_full, preferred_element_type=jnp.float32) + fc_bias_full
    hidden_bf = gelu_value(hidden_pre).astype(jnp.bfloat16)
    mlp_out = jnp.dot(hidden_bf, proj_full, preferred_element_type=jnp.float32)
    hidden_grad = jnp.einsum("td,fd->tf", out_grad, proj_full, preferred_element_type=jnp.float32)
    pre_grad = (hidden_grad * gelu_slope(hidden_pre)).astype(jnp.bfloat16)
    g_proj = jnp.einsum("tf,td->fd", hidden_bf, out_grad, preferred_element_type=jnp.float32)
    g_fc = jnp.einsum("td,tf->df", norm2_bf, pre_grad, preferred_element_type=jnp.float32)
    g_fc_bias = jnp.sum(pre_grad.astype(jnp.float32), axis=0)
    norm2_grad = jnp.einsum("tf,df->td", pre_grad, fc_full, preferred_element_type=jnp.float32)
    block_output = (resid1 + mlp_out + proj_bias_full).astype(jnp.bfloat16)
    g_proj_bias = jnp.sum(grad_vals, axis=0)
    g_mlp_gain = jnp.sum(norm2_grad * normed2, axis=0)
    g_mlp_shift = jnp.sum(norm2_grad, axis=0)
    resid1_grad = grad_vals + norm_backward(norm2_grad, normed2, rstd2, gain2)
    resid1_bf = resid1_grad.astype(jnp.bfloat16)
    g_out = jnp.einsum("td,te->de", attn_tok, resid1_bf, preferred_element_type=jnp.float32)
    g_out_bias = jnp.sum(resid1_grad, axis=0)
    attn_grad = jnp.einsum(
        "te,de->td", resid1_bf, out_full, preferred_element_type=jnp.float32
    ).astype(jnp.bfloat16)
    grad_heads = lax.all_to_all(
        attn_grad.reshape(1, tok_local, groups, group_width),
        "seq",
        split_axis=2,
        concat_axis=0,
        tiled=True,
    )
    dout_r = grad_heads.reshape(groups, tok_local, heads_group, head_size)
    delta_r = jnp.sum(
        dout_r.astype(jnp.float32)
        * out_heads.reshape(groups, tok_local, heads_group, head_size).astype(jnp.float32),
        axis=-1,
    )
    query_every, dout_every = (
        lax.all_gather(query_r, "fsdp", axis=1, tiled=True),
        lax.all_gather(dout_r, "fsdp", axis=1, tiled=True),
    )
    lse_every, delta_every = (
        lax.all_gather(lse_heads, "fsdp", axis=1, tiled=True),
        lax.all_gather(delta_r, "fsdp", axis=1, tiled=True),
    )
    keys_own = kv_own[:, 0, :, 0, :].reshape(groups, tok_local, heads_group, head_size)
    vals_own = kv_own[:, 0, :, 1, :].reshape(groups, tok_local, heads_group, head_size)
    query_span = jnp.arange(piece_len, dtype=jnp.int32)

    def query_piece(q_idx, carry):
        q_blk = lax.dynamic_index_in_dim(query_every, q_idx, 0, keepdims=False)
        d_blk = lax.dynamic_index_in_dim(dout_every, q_idx, 0, keepdims=False)
        l_blk = lax.dynamic_index_in_dim(lse_every, q_idx, 0, keepdims=False)
        e_blk = lax.dynamic_index_in_dim(delta_every, q_idx, 0, keepdims=False)
        q_abs = q_idx * piece_len + query_span

        def own_step(k_idx, inner):
            key_acc, value_acc = inner
            keys_k = lax.dynamic_index_in_dim(keys_own, k_idx, 0, keepdims=False)
            vals_k = lax.dynamic_index_in_dim(vals_own, k_idx, 0, keepdims=False)
            visible = (k_idx * piece_len + row_pos)[None, :] <= q_abs[:, None]
            scores = (
                jnp.einsum("qhd,khd->hqk", q_blk, keys_k, preferred_element_type=jnp.float32)
                * score_scale
            )
            probs = jnp.where(visible[None], jnp.exp(scores - l_blk.T[:, :, None]), 0.0)
            value_part = jnp.einsum(
                "hqk,qhd->khd",
                probs.astype(jnp.bfloat16),
                d_blk,
                preferred_element_type=jnp.float32,
            )
            prob_grad = jnp.einsum(
                "qhd,khd->hqk", d_blk, vals_k, preferred_element_type=jnp.float32
            )
            score_grad = (probs * (prob_grad - e_blk.T[:, :, None])).astype(jnp.bfloat16)
            key_part = (
                jnp.einsum("hqk,qhd->khd", score_grad, q_blk, preferred_element_type=jnp.float32)
                * score_scale
            )
            cur_key = lax.dynamic_index_in_dim(key_acc, k_idx, 0, keepdims=False) + key_part
            cur_value = lax.dynamic_index_in_dim(value_acc, k_idx, 0, keepdims=False) + value_part
            key_acc = lax.dynamic_update_index_in_dim(key_acc, cur_key, k_idx, 0)
            value_acc = lax.dynamic_update_index_in_dim(value_acc, cur_value, k_idx, 0)
            return (key_acc, value_acc)

        return lax.fori_loop(0, q_idx + 1, own_step, carry)

    empty_own = jnp.zeros((groups, tok_local, heads_group, head_size), jnp.float32)
    key_acc, value_acc = lax.fori_loop(0, groups, query_piece, (empty_own, empty_own))

    def query_block(blk_idx, query_grad):
        query_blk = lax.dynamic_slice_in_dim(query_r, 2 * blk_idx, 2, 0).reshape(
            pair_rows, heads_group, head_size
        )
        dout_blk = lax.dynamic_slice_in_dim(dout_r, 2 * blk_idx, 2, 0).reshape(
            pair_rows, heads_group, head_size
        )
        lse_blk = lax.dynamic_slice_in_dim(lse_heads, 2 * blk_idx, 2, 0).reshape(
            pair_rows, heads_group
        )
        delta_blk = lax.dynamic_slice_in_dim(delta_r, 2 * blk_idx, 2, 0).reshape(
            pair_rows, heads_group
        )
        q_pos = query_positions(blk_idx)

        def query_key_step(key_idx, acc):
            kv_blk = lax.dynamic_index_in_dim(kv_pieces, key_idx, 0, keepdims=False)
            visible = (key_idx * piece_len + key_pos)[None, :] <= q_pos[:, None]
            scores = (
                jnp.einsum(
                    "qhd,khd->hqk", query_blk, kv_blk[:, 0], preferred_element_type=jnp.float32
                )
                * score_scale
            )
            probs = jnp.where(visible[None], jnp.exp(scores - lse_blk.T[:, :, None]), 0.0)
            prob_grad = jnp.einsum(
                "qhd,khd->hqk", dout_blk, kv_blk[:, 1], preferred_element_type=jnp.float32
            )
            score_grad = (probs * (prob_grad - delta_blk.T[:, :, None])).astype(jnp.bfloat16)
            return (
                acc
                + jnp.einsum(
                    "hqk,khd->qhd", score_grad, kv_blk[:, 0], preferred_element_type=jnp.float32
                )
                * score_scale
            )

        part = lax.fori_loop(
            0,
            2 * blk_idx + 2,
            query_key_step,
            jnp.zeros((pair_rows, heads_group, head_size), jnp.float32),
        )
        return lax.dynamic_update_slice_in_dim(
            query_grad, part.reshape(2, tok_local, heads_group, head_size), 2 * blk_idx, 0
        )

    query_grad = lax.fori_loop(
        0,
        pair_count,
        query_block,
        jnp.zeros((groups, tok_local, heads_group, head_size), jnp.float32),
    )
    key_grads = jnp.concatenate(
        [
            key_acc.reshape(groups, tok_local, 1, group_width),
            value_acc.reshape(groups, tok_local, 1, group_width),
        ],
        axis=2,
    )
    qkv_grad = jnp.concatenate(
        [query_grad.reshape(groups, tok_local, 1, group_width), key_grads], axis=2
    ).astype(jnp.bfloat16)
    qkv_back = lax.all_to_all(
        qkv_grad.reshape(groups, tok_local, 3, 1, group_width),
        "seq",
        split_axis=0,
        concat_axis=3,
        tiled=True,
    )
    qkv_grad_tok = qkv_back.reshape(tok_local, 3 * width)
    g_qkv = jnp.einsum("td,tc->dc", norm1_bf, qkv_grad_tok, preferred_element_type=jnp.float32)
    qkv_grad_vals = qkv_grad_tok.astype(jnp.float32)
    g_query_bias = jnp.sum(qkv_grad_vals[:, :width], axis=0)
    g_value_bias = jnp.sum(qkv_grad_vals[:, 2 * width :], axis=0)
    norm1_grad = jnp.einsum("tc,dc->td", qkv_grad_tok, qkv_full, preferred_element_type=jnp.float32)
    g_attn_gain = jnp.sum(norm1_grad * normed1, axis=0)
    g_attn_shift = jnp.sum(norm1_grad, axis=0)
    input_grad = resid1_grad + norm_backward(norm1_grad, normed1, rstd1, gain1)
    (
        s_attn_gain,
        s_attn_shift,
        s_qkv,
        s_query_bias,
        s_value_bias,
        s_out,
        s_out_bias,
        s_mlp_gain,
        s_mlp_shift,
        s_fc,
        s_fc_bias,
        s_proj,
        s_proj_bias,
    ) = (
        lax.psum_scatter(
            g_attn_gain.astype(jnp.bfloat16), "fsdp", scatter_dimension=0, tiled=True
        ).astype(jnp.float32),
        lax.psum_scatter(
            g_attn_shift.astype(jnp.bfloat16), "fsdp", scatter_dimension=0, tiled=True
        ).astype(jnp.float32),
        lax.psum_scatter(
            g_qkv.astype(jnp.bfloat16), "fsdp", scatter_dimension=0, tiled=True
        ).astype(jnp.float32),
        lax.psum_scatter(
            g_query_bias.astype(jnp.bfloat16), "fsdp", scatter_dimension=0, tiled=True
        ).astype(jnp.float32),
        lax.psum_scatter(
            g_value_bias.astype(jnp.bfloat16), "fsdp", scatter_dimension=0, tiled=True
        ).astype(jnp.float32),
        lax.psum_scatter(
            g_out.astype(jnp.bfloat16), "fsdp", scatter_dimension=0, tiled=True
        ).astype(jnp.float32),
        lax.psum_scatter(
            g_out_bias.astype(jnp.bfloat16), "fsdp", scatter_dimension=0, tiled=True
        ).astype(jnp.float32),
        lax.psum_scatter(
            g_mlp_gain.astype(jnp.bfloat16), "fsdp", scatter_dimension=0, tiled=True
        ).astype(jnp.float32),
        lax.psum_scatter(
            g_mlp_shift.astype(jnp.bfloat16), "fsdp", scatter_dimension=0, tiled=True
        ).astype(jnp.float32),
        lax.psum_scatter(g_fc.astype(jnp.bfloat16), "fsdp", scatter_dimension=1, tiled=True).astype(
            jnp.float32
        ),
        lax.psum_scatter(
            g_fc_bias.astype(jnp.bfloat16), "fsdp", scatter_dimension=0, tiled=True
        ).astype(jnp.float32),
        lax.psum_scatter(
            g_proj.astype(jnp.bfloat16), "fsdp", scatter_dimension=0, tiled=True
        ).astype(jnp.float32),
        lax.psum_scatter(
            g_proj_bias.astype(jnp.bfloat16), "fsdp", scatter_dimension=0, tiled=True
        ).astype(jnp.float32),
    )
    totals = (
        lax.psum(s_attn_gain.astype(jnp.bfloat16), "seq").astype(jnp.float32),
        lax.psum(s_attn_shift.astype(jnp.bfloat16), "seq").astype(jnp.float32),
        lax.psum(s_qkv.astype(jnp.bfloat16), "seq").astype(jnp.float32),
        lax.psum(s_query_bias.astype(jnp.bfloat16), "seq").astype(jnp.float32),
        lax.psum(s_value_bias.astype(jnp.bfloat16), "seq").astype(jnp.float32),
        lax.psum(s_out.astype(jnp.bfloat16), "seq").astype(jnp.float32),
        lax.psum(s_out_bias.astype(jnp.bfloat16), "seq").astype(jnp.float32),
        lax.psum(s_mlp_gain.astype(jnp.bfloat16), "seq").astype(jnp.float32),
        lax.psum(s_mlp_shift.astype(jnp.bfloat16), "seq").astype(jnp.float32),
        lax.psum(s_fc.astype(jnp.bfloat16), "seq").astype(jnp.float32),
        lax.psum(s_fc_bias.astype(jnp.bfloat16), "seq").astype(jnp.float32),
        lax.psum(s_proj.astype(jnp.bfloat16), "seq").astype(jnp.float32),
        lax.psum(s_proj_bias.astype(jnp.bfloat16), "seq").astype(jnp.float32),
    )
    return (block_output, input_grad) + tuple(totals)


def solution(mesh):
    return jax.shard_map(
        on_device,
        mesh=mesh,
        in_specs=(
            P(("seq", "fsdp"), None),
            P(("seq", "fsdp"), None),
            P("fsdp"),
            P("fsdp"),
            P("fsdp", None),
            P("fsdp"),
            P("fsdp"),
            P("fsdp", None),
            P("fsdp"),
            P("fsdp"),
            P("fsdp"),
            P(None, "fsdp"),
            P("fsdp"),
            P("fsdp", None),
            P("fsdp"),
        ),
        out_specs=(
            P(("seq", "fsdp"), None),
            P(("seq", "fsdp"), None),
            P("fsdp"),
            P("fsdp"),
            P("fsdp", None),
            P("fsdp"),
            P("fsdp"),
            P("fsdp", None),
            P("fsdp"),
            P("fsdp"),
            P("fsdp"),
            P(None, "fsdp"),
            P("fsdp"),
            P("fsdp", None),
            P("fsdp"),
        ),
        check_vma=False,
    )
```

profile of v0, /device:TPU:0, one launch (start us, length us, event | category | flops | bytes accessed | tf_op | source)
XLA Modules:
  0.0 726.8 jit_solution(18390651284466168723)
XLA Ops:
  8.0 10.4 %all-gather.4 = bf16[8,1,128]{2,1,0:T(2,128)(2,1)S(1)} all-gather(bf16[1,1,128]{2,1,0:T(2,128)(2,1)} %bitcast.368), channel_id=1, replica_groups=mesh['seq'=4,'fsdp'=8] {'fsdp'}, dimensions={0}, use_global_device_ids=true | all-gather | bytes 2304 | tf_op jit(solution)/shard_map/all_gather | solution.py:81
  18.4 8.8 %all-gather.3 = bf16[8,1,128]{2,1,0:T(2,128)(2,1)S(1)} all-gather(bf16[1,1,128]{2,1,0:T(2,128)(2,1)} %bitcast.369), channel_id=1, replica_groups=mesh['seq'=4,'fsdp'=8] {'fsdp'}, dimensions={0}, use_global_device_ids=true | all-gather | bytes 2304 | tf_op jit(solution)/shard_map/all_gather | solution.py:80
  27.1 8.1 %all-gather.2 = bf16[8,1,128]{2,1,0:T(2,128)(2,1)S(1)} all-gather(bf16[1,1,128]{2,1,0:T(2,128)(2,1)} %bitcast.370), channel_id=1, replica_groups=mesh['seq'=4,'fsdp'=8] {'fsdp'}, dimensions={0}, use_global_device_ids=true | all-gather | bytes 2304 | tf_op jit(solution)/shard_map/all_gather | solution.py:78
  35.2 8.6 %all-gather.1 = bf16[8,1,128]{2,1,0:T(2,128)(2,1)S(1)} all-gather(bf16[1,1,128]{2,1,0:T(2,128)(2,1)} %bitcast.371), channel_id=1, replica_groups=mesh['seq'=4,'fsdp'=8] {'fsdp'}, dimensions={0}, use_global_device_ids=true | all-gather | bytes 2304 | tf_op jit(solution)/shard_map/all_gather | solution.py:77
  46.2 11.9 %all-gather.18.cloned.1.call-done = bf16[1024,3072]{1,0:T(8,128)(2,1)} async-done(((bf16[128,3072]{1,0:T(8,128)(2,1)}), bf16[1024,3072]{1,0:T(8,128)(2,1)}) %all-gather.18.cloned.1.call-update) | async-done | bytes 6291472 | tf_op jit(solution)/shard_map/all_gather | solution.py:79
  58.1 4.0 fusion.62
  63.5 24.9 %all_to_all.63 = bf16[1,128,3,4,256]{1,4,2,0,3:T(8,128)(2,1)S(1)} all-to-all(bf16[1,128,3,4,256]{1,4,2,0,3:T(8,128)(2,1)S(1)} %copy.86), channel_id=1, replica_groups=mesh['seq'=4,'fsdp'=8] {'seq'}, dimensions={3} | all-to-all | bytes 1572864 | tf_op jit(solution)/shard_map/all_to_all | solution.py:115
  91.8 33.5 %all-gather.30.cloned.1.call-done = bf16[4,1024,2,1,256]{1,4,0,2,3:T(8,128)(2,1)} async-done(((bf16[4,128,2,1,256]{1,4,0,2,3:T(8,128)(2,1)}), bf16[4,1024,2,1,256]{1,4,0,2,3:T(8,128)(2,1)}) %all-gather.30.cloned.1.call-update) | async-done | bytes 4194320 | tf_op jit(solution)/shard_map/all_gather | solution.py:124
  125.3 4.8 copy.89
  130.3 23.6 %while.126 = (s32[]{:T(128)}, bf16[4,128,256]{1,0,2:T(4,128)(2,1)S(1)}, f32[4,128,4]{1,0,2:T(4,128)S(1)}, bf16[4,128,4,64]{1,0,3,2:T(4,128)(2,1)S(1)}, bf16[4,10...) while((s32[]{:T(128)}, ...), condition=%wide.region_6.7_spmd.clone, body=%wide.region_2.6_spmd.clone.sunk | while | flops 275187072 | bytes 14749222 | solution.py:175
  130.6 7.5 %while.131 = (s32[]{:T(128)}, f32[256,4,64]{0,2,1:T(8,128)S(1)}, f32[4,256]{1,0:T(4,128)S(1)}, s32[]{:T(128)}, bf16[4,1024,2,4,64]{1,4,3,2,0:T(8,128)(2,1)}, /*i...) while((s32[]{:T(128)}, f32[256,4,64]{0,2,1:T(8,128)S(1)}, ...), condition=%wide.region_5.5_spmd.clone, body=%wide.region_3.4_spmd.clone.sunk | while | flops 275055872 | bytes 13007555 | solution.py:165
  138.7 14.8 %while.131 = (s32[]{:T(128)}, f32[256,4,64]{0,2,1:T(8,128)S(1)}, f32[4,256]{1,0:T(4,128)S(1)}, s32[]{:T(128)}, bf16[4,1024,2,4,64]{1,4,3,2,0:T(8,128)(2,1)}, /*i...) while((s32[]{:T(128)}, f32[256,4,64]{0,2,1:T(8,128)S(1)}, ...), condition=%wide.region_5.5_spmd.clone, body=%wide.region_3.4_spmd.clone.sunk | while | flops 275055872 | bytes 13007555 | solution.py:165
  154.6 4.5 all-to-all-start.1
  159.1 8.7 %all-gather.5 = bf16[8,1,128]{2,1,0:T(2,128)(2,1)S(1)} all-gather(bf16[1,1,128]{2,1,0:T(2,128)(2,1)S(1)} %bitcast.372), channel_id=1, replica_groups=mesh['seq'=4,'fsdp'=8] {'fsdp'}, dimensions={0}, use_global_device_ids=true | all-gather | bytes 2304 | tf_op jit(solution)/shard_map/all_gather | solution.py:83
  167.9 8.6 %all-gather.8 = bf16[8,1,512]{2,1,0:T(2,128)(2,1)S(1)} all-gather(bf16[1,1,512]{2,1,0:T(2,128)(2,1)S(1)} %reshape.355), channel_id=1, replica_groups=mesh['seq'=4,'fsdp'=8] {'fsdp'}, dimensions={0}, use_global_device_ids=true | all-gather | bytes 9216 | tf_op jit(solution)/shard_map/all_gather | solution.py:87
  176.5 8.5 %all-gather.7 = bf16[8,1,128]{2,1,0:T(2,128)(2,1)S(1)} all-gather(bf16[1,1,128]{2,1,0:T(2,128)(2,1)S(1)} %bitcast.373), channel_id=1, replica_groups=mesh['seq'=4,'fsdp'=8] {'fsdp'}, dimensions={0}, use_global_device_ids=true | all-gather | bytes 2304 | tf_op jit(solution)/shard_map/all_gather | solution.py:85
  185.0 8.4 %all-gather.6 = bf16[8,1,128]{2,1,0:T(2,128)(2,1)S(1)} all-gather(bf16[1,1,128]{2,1,0:T(2,128)(2,1)S(1)} %bitcast.374), channel_id=1, replica_groups=mesh['seq'=4,'fsdp'=8] {'fsdp'}, dimensions={0}, use_global_device_ids=true | all-gather | bytes 2304 | tf_op jit(solution)/shard_map/all_gather | solution.py:84
  196.2 16.6 %all-gather.22.cloned.1.call-done = bf16[1024,4096]{1,0:T(8,128)(2,1)} async-done(((bf16[1024,512]{1,0:T(8,128)(2,1)}), bf16[1024,4096]{1,0:T(8,128)(2,1)}) %all-gather.22.cloned.1.call-update) | async-done | bytes 8388624 | tf_op jit(solution)/shard_map/all_gather | solution.py:86
  212.7 4.8 convolution_add_fusion
  217.5 51.2 %all-gather.24.cloned.1.call-done = bf16[4096,1024]{1,0:T(8,128)(2,1)} async-done(((bf16[512,1024]{1,0:T(8,128)(2,1)}), bf16[4096,1024]{1,0:T(8,128)(2,1)}) %all-gather.24.cloned.1.call-update) | async-done | bytes 8388624 | tf_op jit(solution)/shard_map/all_gather | solution.py:88
  268.7 7.7 %fusion.92 = (bf16[4096]{0:T(1024)(128)(2,1)}, bf16[128,4096]{1,0:T(8,128)(2,1)S(1)}) fusion(f32[128,4096]{1,0:T(8,128)S(1)} %convolution_add_fusion, bf16[128,1024]{1,0:T(8,128)(2,1)S(1)} %copy-done.13, bf16[4096,1024]{1,0:T(8,128)(2,1)} %all-gather.24.cloned.1.call-done), kind=kOutput, calls=%fused_computation.157 | convolution fusion | flops 1084223488 | bytes 11804672 | tf_op jit(solution)/shard_map/td,fd->tf/dot_general | solution.py:200
  276.4 3.5 multiply_reduce_fusion
  285.2 13.8 %all_to_all.64 = bf16[1,128,4,256]{3,1,0,2:T(8,128)(2,1)} all-to-all(bf16[1,128,4,256]{3,1,0,2:T(8,128)(2,1)S(1)} %copy.91), channel_id=1, replica_groups=mesh['seq'=4,'fsdp'=8] {'seq'}, dimensions={2} | all-to-all | bytes 524288 | tf_op jit(solution)/shard_map/all_to_all | solution.py:217
  300.8 3.0 convolution_convert_fusion.3
  303.9 6.9 convolution_convert_fusion.1
  312.7 9.1 %all_gather.69 = f32[4,1024,4]{1,2,0:T(4,128)S(1)} all-gather(f32[4,128,4]{1,2,0:T(4,128)S(1)} %copy.100), channel_id=1, replica_groups=mesh['seq'=4,'fsdp'=8] {'fsdp'}, dimensions={1}, use_global_device_ids=true | all-gather | bytes 73728 | tf_op jit(solution)/shard_map/all_gather | solution.py:235
  321.8 5.7 convolution_convert_fusion
  328.5 9.0 %all_gather.71 = f32[4,1024,4]{1,2,0:T(4,128)} all-gather(f32[4,128,4]{1,2,0:T(4,128)S(1)} %multiply_reduce_fusion.1), channel_id=1, replica_groups=mesh['seq'=4,'fsdp'=8] {'fsdp'}, dimensions={1}, use_global_device_ids=true | all-gather | bytes 73728 | tf_op jit(solution)/shard_map/all_gather | solution.py:236
  337.6 52.8 %while.128 = (s32[]{:T(128)}, bf16[4,128,4,64]{1,0,3,2:T(4,128)(2,1)S(1)}, bf16[4,128,4,64]{1,0,3,2:T(4,128)(2,1)S(1)}, f32[4,128,4]{1,0,2:T(4,128)S(1)}, bf16[4...) while((s32[]{:T(128)}, ...), condition=%wide.region_15.16_spmd.clone, body=%wide.region_12.0_spmd.clone.sunk | while | flops 409339264 | bytes 15126106 | solution.py:331
  338.0 17.0 %while.132 = (s32[]{:T(128)}, f32[256,4,64]{0,2,1:T(8,128)S(1)}, s32[]{:T(128)}, bf16[4,1024,2,4,64]{1,4,3,2,0:T(8,128)(2,1)}, s32[1024]{0:T(1024)S(1)}, /*index...) while((s32[]{:T(128)}, f32[256,4,64]{0,2,1:T(8,128)S(1)}, ...), condition=%wide.region_14.14_spmd.clone, body=%wide.region_13.13_spmd.clone.sunk | while | flops 409339136 | bytes 13392595 | solution.py:321
  339.4 2.7 fusion.144
  342.4 4.2 fusion.145
  348.0 2.7 fusion.144
  351.0 4.0 fusion.145
  355.7 34.5 %while.132 = (s32[]{:T(128)}, f32[256,4,64]{0,2,1:T(8,128)S(1)}, s32[]{:T(128)}, bf16[4,1024,2,4,64]{1,4,3,2,0:T(8,128)(2,1)}, s32[1024]{0:T(1024)S(1)}, /*index...) while((s32[]{:T(128)}, f32[256,4,64]{0,2,1:T(8,128)S(1)}, ...), condition=%wide.region_14.14_spmd.clone, body=%wide.region_13.13_spmd.clone.sunk | while | flops 409339136 | bytes 13392595 | solution.py:321
  357.0 2.7 fusion.144
  360.0 4.0 fusion.145
  365.4 2.7 fusion.144
  368.5 4.0 fusion.145
  373.8 2.7 fusion.144
  376.9 4.0 fusion.145
  382.2 2.7 fusion.144
  385.3 4.9 fusion.145
  392.9 70.3 %while.130 = (s32[]{:T(128)}, f32[4,128,4,64]{1,3,2,0:T(8,128)}, f32[4,128,4,64]{1,3,2,0:T(8,128)}, bf16[4,1024,4,64]{1,3,2,0:T(8,128)(2,1)}, f32[4,1024,4]{1,2,...) while((s32[]{:T(128)}, f32[4,128,4,64]{1,3,2,0:T(8,128)}, ...), condition=%wide.region_19.20_spmd.clone, body=%wide.region_16.0_spmd.clone.sunk | while | flops 272336128 | bytes 12037668 | solution.py:282
  395.0 6.2 while.133
  403.3 12.4 %while.133 = (s32[]{:T(128)}, f32[4,128,4,64]{1,3,2,0:T(8,128)}, f32[4,128,4,64]{1,3,2,0:T(8,128)}, s32[]{:T(128)}, s32[128]{0:T(128)S(1)}, /*index=5*/s32[1024]...) while((s32[]{:T(128)}, f32[4,128,4,64]{1,3,2,0:T(8,128)}, ...), condition=%wide.region_18.18_spmd, body=%wide.region_17.17_spmd.sunk | while | flops 272334976 | bytes 9870043 | solution.py:279
  406.0 2.3 fusion.140
  412.2 2.3 fusion.140
  417.7 18.6 %while.133 = (s32[]{:T(128)}, f32[4,128,4,64]{1,3,2,0:T(8,128)}, f32[4,128,4,64]{1,3,2,0:T(8,128)}, s32[]{:T(128)}, s32[128]{0:T(128)S(1)}, /*index=5*/s32[1024]...) while((s32[]{:T(128)}, f32[4,128,4,64]{1,3,2,0:T(8,128)}, ...), condition=%wide.region_18.18_spmd, body=%wide.region_17.17_spmd.sunk | while | flops 272334976 | bytes 9870043 | solution.py:279
  420.4 2.3 fusion.140
  438.3 24.8 %while.133 = (s32[]{:T(128)}, f32[4,128,4,64]{1,3,2,0:T(8,128)}, f32[4,128,4,64]{1,3,2,0:T(8,128)}, s32[]{:T(128)}, s32[128]{0:T(128)S(1)}, /*index=5*/s32[1024]...) while((s32[]{:T(128)}, f32[4,128,4,64]{1,3,2,0:T(8,128)}, ...), condition=%wide.region_18.18_spmd, body=%wide.region_17.17_spmd.sunk | while | flops 272334976 | bytes 9870043 | solution.py:279
  447.3 2.3 fusion.140
  459.7 2.3 fusion.140
  466.7 23.3 %all_to_all.65 = bf16[4,128,3,1,256]{1,4,3,2,0:T(8,128)(2,1)S(1)} all-to-all(bf16[4,128,3,1,256]{1,4,3,2,0:T(8,128)(2,1)S(1)} %pad_maximum_fusion), channel_id=1, replica_groups=mesh['seq'=4,'fsdp'=8] {'seq'}, dimensions={0} | all-to-all | bytes 1572864 | tf_op jit(solution)/shard_map/all_to_all | solution.py:347
  491.0 4.7 convolution_convert_fusion.2
  495.9 27.9 %reduce-scatter.11.cloned.1.call-done = bf16[512,1024]{1,0:T(8,128)(2,1)} async-done(((bf16[4096,1024]{1,0:T(8,128)(2,1)}), bf16[512,1024]{1,0:T(8,128)(2,1)}) %reduce-scatter.11.cloned.1.call-update) | async-done | bytes 1048592 | tf_op jit(solution)/shard_map/reduce_scatter | solution.py:411
  523.8 65.2 %reduce-scatter.5.cloned.1.call-done = bf16[128,3072]{1,0:T(8,128)(2,1)} async-done(((bf16[1024,3072]{1,0:T(8,128)(2,1)}), bf16[128,3072]{1,0:T(8,128)(2,1)}) %reduce-scatter.5.cloned.1.call-update) | async-done | bytes 786448 | tf_op jit(solution)/shard_map/reduce_scatter | solution.py:384
  589.1 9.1 %all-gather.9 = bf16[8,1,128]{2,1,0:T(2,128)(2,1)S(1)} all-gather(bf16[1,1,128]{2,1,0:T(2,128)(2,1)S(1)} %bitcast.375), channel_id=1, replica_groups=mesh['seq'=4,'fsdp'=8] {'fsdp'}, dimensions={0}, use_global_device_ids=true | all-gather | bytes 2304 | tf_op jit(solution)/shard_map/all_gather | solution.py:89
  600.1 6.4 fusion.70
  607.1 2.4 fusion.83
  609.5 25.2 %all-reduce.9 = (bf16[1024]{0:T(1024)(128)(2,1)S(1)}, bf16[1024]{0:T(1024)(128)(2,1)S(1)}, bf16[1024]{0:T(1024)(128)(2,1)S(1)}, bf16[1024]{0:T(1024)(128)(2,1)S(...) all-reduce(bf16[1024]{0:T(1024)(128)(2,1)S(1)} %get-tuple-element.8, ...), channel_id=3, replica_groups=mesh['seq'=4,'fsdp'=8] {'fsdp'}, use_global_device_ids=true, to_apply=%region_23.24.clone | all-reduce | flops 12288 | bytes 49152
  635.4 12.7 %all-reduce.10 = (bf16[128]{0:T(256)(128)(2,1)S(1)}, bf16[128]{0:T(256)(128)(2,1)S(1)}, bf16[128]{0:T(256)(128)(2,1)S(1)}, bf16[128]{0:T(256)(128)(2,1)S(1)}, bf...) all-reduce(bf16[128]{0:T(256)(128)(2,1)S(1)} %dynamic-slice.1, ...), channel_id=1, replica_groups=mesh['seq'=4,'fsdp'=8] {'seq'}, use_global_device_ids=true, to_apply=%region_24.25 | all-reduce | flops 1536 | bytes 6144 | tf_op jit(solution)/shard_map/psum | solution.py:419
  653.8 59.2 %all-reduce.14.cloned.1.call-done = (bf16[128,3072]{1,0:T(8,128)(2,1)}, bf16[128,1024]{1,0:T(8,128)(2,1)}, bf16[1024,512]{1,0:T(8,128)(2,1)}, bf16[512,1024]{1,0:T(8,128)(2,1)}) async-done(((bf16[128,3072]{1,0:T(8,128)(2,1)}, bf16[128,1024]{1,0:T(8,128)(2,1)}, bf16[1024,512]{1,0:T(8,128)(2,1)}, bf16[512,1024]{1,0:T(8,128)(2,1)}), (bf16[128,3072]{1,0:T(8,128)(2,1)}, bf16[128,1024]{1,0:T(8,128)(2,1)}, ...) | async-done | bytes 3145744 | tf_op jit(solution)/shard_map/psum | solution.py:421
  713.0 2.5 convert_element_type.232
  (383 shorter events, 132.4 us)
Async XLA Ops:
  7.2 50.9 %all-gather.18.cloned.1.call-start = ((), (), s32[]{:S(2)}) async-start(), calls=%async_computation.8 | async-start | bytes 7077888 | tf_op jit(solution)/shard_map/all_gather | solution.py:79
  7.9 117.4 %all-gather.30.cloned.1.call-start = ((), (), s32[]{:S(2)}) async-start(), calls=%async_computation.18 | async-start | bytes 4718592 | tf_op jit(solution)/shard_map/all_gather | solution.py:124
  35.2 22.8 %copy-start.26 = (f32[8,1,128]{2,1,0:T(1,128)}, f32[8,1,128]{2,1,0:T(1,128)S(1)}, u32[]{:S(2)}) copy-start(f32[8,1,128]{2,1,0:T(1,128)S(1)} %convert_element_type.254) | copy-start | bytes 12292
  43.9 14.2 %copy-start.24 = (f32[8,1,128]{2,1,0:T(1,128)}, f32[8,1,128]{2,1,0:T(1,128)S(1)}, u32[]{:S(2)}) copy-start(f32[8,1,128]{2,1,0:T(1,128)S(1)} %convert_element_type.253) | copy-start | bytes 12292
  45.0 13.1 %copy-start.29 = (f32[128]{0:T(128)}, f32[128]{0:T(128)S(1)}, u32[]{:S(2)}) copy-start(f32[128]{0:T(128)S(1)} %broadcast_multiply_fusion.5) | copy-start | bytes 1540
  46.1 11.9 %copy-start.31 = (f32[128]{0:T(128)}, f32[128]{0:T(128)S(1)}, u32[]{:S(2)}) copy-start(f32[128]{0:T(128)S(1)} %add_rsqrt_fusion.1) | copy-start | bytes 1540
  89.7 104.0 %all-gather.20.cloned.1.call-start = ((), (), s32[]{:S(2)}) async-start(), calls=%async_computation.9 | async-start | bytes 2359296 | tf_op jit(solution)/shard_map/all_gather | solution.py:82
  90.4 122.3 %all-gather.22.cloned.1.call-start = ((), (), s32[]{:S(2)}) async-start(), calls=%async_computation.10 | async-start | bytes 9437184 | tf_op jit(solution)/shard_map/all_gather | solution.py:86
  91.0 177.8 %all-gather.24.cloned.1.call-start = ((), (), s32[]{:S(2)}) async-start(), calls=%async_computation.11 | async-start | bytes 9437184 | tf_op jit(solution)/shard_map/all_gather | solution.py:88
  91.6 38.5 %copy-start.19 = (bf16[4,128,1,1,256]{1,4,0,2,3:T(8,128)(2,1)}, bf16[4,128,1,1,256]{1,4,0,2,3:T(8,128)(2,1)S(1)}, u32[]{:S(2)}) copy-start(bf16[4,128,1,1,256]{1,4,0,2,3:T(8,128)(2,1)S(1)} %slice.45) | copy-start | bytes 786436
  130.2 28.9 %copy-start.38 = (bf16[128]{0:T(256)(128)(2,1)S(1)}, bf16[128]{0:T(256)(128)(2,1)}, u32[]{:S(2)}) copy-start(bf16[128]{0:T(256)(128)(2,1)} %param.35) | copy-start | bytes 772
  130.2 37.7 %copy-start.37 = (bf16[512]{0:T(512)(128)(2,1)S(1)}, bf16[512]{0:T(512)(128)(2,1)}, u32[]{:S(2)}) copy-start(bf16[512]{0:T(512)(128)(2,1)} %param.39) | copy-start | bytes 3076
  130.2 46.3 %copy-start.39 = (bf16[128]{0:T(256)(128)(2,1)S(1)}, bf16[128]{0:T(256)(128)(2,1)}, u32[]{:S(2)}) copy-start(bf16[128]{0:T(256)(128)(2,1)} %param.37) | copy-start | bytes 772
  130.2 54.7 %copy-start.40 = (bf16[128]{0:T(256)(128)(2,1)S(1)}, bf16[128]{0:T(256)(128)(2,1)}, u32[]{:S(2)}) copy-start(bf16[128]{0:T(256)(128)(2,1)} %param.36) | copy-start | bytes 772
  130.2 63.4 %copy-start.3 = (bf16[128,1024]{1,0:T(8,128)(2,1)S(1)}, bf16[128,1024]{1,0:T(8,128)(2,1)}, u32[]{:S(2)}) copy-start(bf16[128,1024]{1,0:T(8,128)(2,1)} %param.27) | copy-start | bytes 786436
  153.8 42.1 %copy-start.17 = (bf16[4,128,256]{1,0,2:T(4,128)(2,1)}, bf16[4,128,256]{1,0,2:T(4,128)(2,1)S(1)}, u32[]{:S(2)}) copy-start(bf16[4,128,256]{1,0,2:T(4,128)(2,1)S(1)} %get-tuple-element.644) | copy-start | bytes 786436
  154.6 39.0 %all-to-all-start.1 = ((bf16[4,128,1,256]{1,3,2,0:T(8,128)(2,1)}), bf16[4,128,1,256]{1,3,2,0:T(8,128)(2,1)S(1)}, u32[]{:S(2)}, u32[]{:S(2)}) async-start(bf16[4,128,1,256]{1,3,2,0:T(8,128)(2,1)} %bitcast.235), calls=%async_computation.1 | async-start | bytes 524288 | tf_op jit(solution)/shard_map/all_to_all | solution.py:184
  159.1 232.1 %all-gather.26.cloned.1.call-start = ((), (), s32[]{:S(2)}) async-start(), calls=%async_computation.12 | async-start | bytes 2359296 | tf_op jit(solution)/shard_map/all_gather | solution.py:231
  193.4 197.8 %all-gather.28.cloned.1.call-start = ((), (), s32[]{:S(2)}) async-start(), calls=%async_computation.13 | async-start | bytes 2359296 | tf_op jit(solution)/shard_map/all_gather | solution.py:232
  193.7 19.1 %copy-start.20 = (bf16[4,128,1,256]{1,3,2,0:T(8,128)(2,1)}, bf16[4,128,1,256]{1,3,2,0:T(8,128)(2,1)S(1)}, u32[]{:S(2)}) copy-start(bf16[4,128,1,256]{1,3,2,0:T(8,128)(2,1)S(1)} %all-to-all-done.1) | copy-start | bytes 786436
  195.9 107.9 %copy-start.1 = (f32[128,1024]{1,0:T(8,128)}, f32[128,1024]{1,0:T(8,128)S(1)}, u32[]{:S(2)}) copy-start(f32[128,1024]{1,0:T(8,128)S(1)} %get-tuple-element.1011) | copy-start | bytes 1572868
  212.7 56.0 %copy-start.13 = (bf16[128,1024]{1,0:T(8,128)(2,1)S(1)}, bf16[128,1024]{1,0:T(8,128)(2,1)}, u32[]{:S(2)}) copy-start(bf16[128,1024]{1,0:T(8,128)(2,1)} %param.28) | copy-start | bytes 786436
  217.5 104.3 %copy-start.5 = (f32[128,4096]{1,0:T(8,128)}, f32[128,4096]{1,0:T(8,128)S(1)}, u32[]{:S(2)}) copy-start(f32[128,4096]{1,0:T(8,128)S(1)} %convolution_add_fusion) | copy-start | bytes 6291460
  268.7 7.7 %copy-start = (bf16[1024,4096]{1,0:T(8,128)(2,1)S(1)}, bf16[1024,4096]{1,0:T(8,128)(2,1)}, u32[]{:S(2)}) copy-start(bf16[1024,4096]{1,0:T(8,128)(2,1)} %all-gather.22.cloned.1.call-done) | copy-start | bytes 25165828
  276.4 3.5 copy-start.12
  276.4 3.5 copy-start.14
  276.4 4.4 copy-start.8
  280.8 20.0 %copy-start.9 = (f32[128,1024]{1,0:T(8,128)}, f32[128,1024]{1,0:T(8,128)S(1)}, u32[]{:S(2)}) copy-start(f32[128,1024]{1,0:T(8,128)S(1)} %get-tuple-element.997) | copy-start | bytes 1572868
  300.8 195.1 %reduce-scatter.7.cloned.1.call-start = ((), (), s32[]{:S(2)}) async-start(), calls=%async_computation.15 | async-start | bytes 2359296 | tf_op jit(solution)/shard_map/reduce_scatter | solution.py:393
  303.8 192.0 %reduce-scatter.9.cloned.1.call-start = ((), (), s32[]{:S(2)}) async-start(), calls=%async_computation.16 | async-start | bytes 9437184 | tf_op jit(solution)/shard_map/reduce_scatter | solution.py:405
  310.8 1.0 copy-start.21
  310.8 1.9 copy-start.18
  310.8 11.0 %copy-start.15 = (bf16[128,1024]{1,0:T(8,128)(2,1)S(1)}, bf16[128,1024]{1,0:T(8,128)(2,1)}, u32[]{:S(2)}) copy-start(bf16[128,1024]{1,0:T(8,128)(2,1)} %param.28) | copy-start | bytes 786436
  310.8 213.0 %reduce-scatter.11.cloned.1.call-start = ((), (), s32[]{:S(2)}) async-start(), calls=%async_computation.17 | async-start | bytes 9437184 | tf_op jit(solution)/shard_map/reduce_scatter | solution.py:411
  327.5 0.9 copy-start.11
  327.5 261.4 %reduce-scatter.5.cloned.1.call-start = ((), (), s32[]{:S(2)}) async-start(), calls=%async_computation.14 | async-start | bytes 7077888 | tf_op jit(solution)/shard_map/reduce_scatter | solution.py:384
  465.5 25.5 %copy-start.4 = (bf16[128,1024]{1,0:T(8,128)(2,1)S(1)}, bf16[128,1024]{1,0:T(8,128)(2,1)}, u32[]{:S(2)}) copy-start(bf16[128,1024]{1,0:T(8,128)(2,1)} %param.27) | copy-start | bytes 786436
  465.5 25.4 %copy-start.25 = (f32[8,1,128]{2,1,0:T(1,128)S(1)}, f32[8,1,128]{2,1,0:T(1,128)}, u32[]{:S(2)}) copy-start(f32[8,1,128]{2,1,0:T(1,128)} %copy-done.24) | copy-start | bytes 12292
  465.5 25.4 %copy-start.27 = (f32[8,1,128]{2,1,0:T(1,128)S(1)}, f32[8,1,128]{2,1,0:T(1,128)}, u32[]{:S(2)}) copy-start(f32[8,1,128]{2,1,0:T(1,128)} %copy-done.26) | copy-start | bytes 12292
  465.6 25.4 %copy-start.30 = (f32[128]{0:T(128)S(1)}, f32[128]{0:T(128)}, u32[]{:S(2)}) copy-start(f32[128]{0:T(128)} %copy-done.29) | copy-start | bytes 1540
  465.6 25.4 %copy-start.32 = (f32[128]{0:T(128)S(1)}, f32[128]{0:T(128)}, u32[]{:S(2)}) copy-start(f32[128]{0:T(128)} %copy-done.31) | copy-start | bytes 1540
  490.1 0.9 copy-start.6
  495.7 93.3 %copy-start.16 = (bf16[128,1024]{1,0:T(8,128)(2,1)S(1)}, bf16[128,1024]{1,0:T(8,128)(2,1)}, u32[]{:S(2)}) copy-start(bf16[128,1024]{1,0:T(8,128)(2,1)} %param.28) | copy-start | bytes 786436
  495.7 93.3 %copy-start.41 = (bf16[128]{0:T(256)(128)(2,1)S(1)}, bf16[128]{0:T(256)(128)(2,1)}, u32[]{:S(2)}) copy-start(bf16[128]{0:T(256)(128)(2,1)} %param.41) | copy-start | bytes 772
  495.7 102.5 %copy-start.42 = (u32[32]{0:T(128)S(1)}, u32[32]{0:T(128)}, u32[]{:S(2)}) copy-start(u32[32]{0:T(128)} %constant.217) | copy-start | bytes 388
  495.7 104.3 %copy-start.2 = (f32[128,1024]{1,0:T(8,128)S(1)}, f32[128,1024]{1,0:T(8,128)}, u32[]{:S(2)}) copy-start(f32[128,1024]{1,0:T(8,128)} %copy-done.1) | copy-start | bytes 1572868
  495.8 217.2 %all-reduce.14.cloned.1.call-start = ((), (), s32[]{:S(2)}) async-start(), calls=%async_computation.19 | async-start | bytes 6291456 | tf_op jit(solution)/shard_map/psum | solution.py:421
  589.0 18.0 %slice-start = ((s8[6291456]{0:T(1024)(128)(4,1)}), s8[2097152]{0:T(1024)(128)(4,1)S(1)}, s32[]{:S(2)}) async-start(s8[6291456]{0:T(1024)(128)(4,1)} %bitcast.326), calls=%async_computation.20 | async-start | bytes 4194304
  600.1 6.4 copy-start.7
  600.1 6.9 slice-start.1
  607.0 2.4 copy-start.33
  607.0 2.4 copy-start.34
  607.0 2.4 copy-start.35
  607.1 2.4 copy-start.36
  607.1 45.7 %copy-start.10 = (f32[128,1024]{1,0:T(8,128)S(1)}, f32[128,1024]{1,0:T(8,128)}, u32[]{:S(2)}) copy-start(f32[128,1024]{1,0:T(8,128)} %copy-done.9) | copy-start | bytes 1572868
  713.0 2.5 copy-start.28
  713.0 3.4 copy-start.23
  715.5 2.5 copy-start.22
Sparse Core Ops, SparseCore 0:
  9.9 48.1 all-gather.17
  89.8 35.4 all-gather.29
  127.2 27.8 all-gather.19
  156.8 55.9 all-gather.21
  214.5 54.2 all-gather.23
  270.5 28.0 all-gather.25
  301.1 28.0 all-gather.27
  333.0 41.0 reduce-scatter.6
  377.6 71.2 reduce-scatter.8
  452.3 71.4 reduce-scatter.10
  527.2 61.7 reduce-scatter.4
  591.4 121.4 all-reduce.13
where the time goes:
time: 736 us; the launch traced here: 727 us
  waiting for transfers between devices  268 us (36%)
  blocking collectives  197 us (27%)
  matrix products  157 us (21%)
  local copies, waits for them, and re-layouts  56.9 us (8%)
  other arithmetic  24.8 us (3%)
  between operations  16.6 us (2%)
    reduce_scatter x1, waiting for transfers between devices, on_device(): lax.psum_scatter(g_qkv.astype(jnp.bfloat16), 'fsdp', scatter_dimension=0,...  65.2 us
    psum x1, waiting for transfers between devices, on_device(): lax.psum(s_qkv.astype(jnp.bfloat16), 'seq').astype(jnp.float32)  59.2 us
    all_gather x1, waiting for transfers between devices, on_device(): lax.all_gather(proj_weight, 'fsdp', axis=0, tiled=True)  51.2 us
    all_gather x1, waiting for transfers between devices, on_device(): kv_all = lax.all_gather(kv_own, 'fsdp', axis=1, tiled=True)  33.5 us
    reduce_scatter x1, waiting for transfers between devices, on_device(): lax.psum_scatter(g_proj.astype(jnp.bfloat16), 'fsdp', scatter_dimension=0...  27.9 us
    unnamed x1, blocking collectives  25.2 us
    dot_general x6, matrix products, query_key_step(): jnp.einsum('hqk,khd->qhd', score_grad, kv_blk[:, 0], preferred_element_ty...  25.1 us
    all_to_all x1, blocking collectives, on_device(): lax.all_to_all(qkv_bf.reshape(1, tok_local, 3, groups, group_width), 'seq...  24.9 us
  transfers between devices with their start and end apart: 13, of which 7 were waited for; matrix products, arithmetic and copies ran while one was open for 31% of the time, Pallas kernels for 0%

commit v1 on v0

v1 whole, which is shorter than its diff:
```python
import functools
import math

import jax
import jax.numpy as jnp
from jax import lax
from jax.experimental import pallas as pl
from jax.experimental.pallas import tpu as pltpu
from jax.sharding import PartitionSpec as P

HEADS = 16
MESH = pl.DeviceIdType.MESH
BF = jnp.bfloat16
F32 = jnp.float32

norm_eps = 1e-05
gelu_coef = 0.7978845608028654
cubic_coef = 0.044715


def norm_stats(values):
    centre = jnp.mean(values, axis=-1, keepdims=True)
    centred = values - centre
    inv_scale = lax.rsqrt(jnp.mean(centred * centred, axis=-1, keepdims=True) + norm_eps)
    return centred * inv_scale, inv_scale


def norm_backward(upstream, normed, inv_scale, gain_vec):
    scaled = upstream * gain_vec
    return inv_scale * (
        scaled
        - jnp.mean(scaled, axis=-1, keepdims=True)
        - normed * jnp.mean(scaled * normed, axis=-1, keepdims=True)
    )


def peer_barrier(n, me, everyone):
    barrier = pltpu.get_barrier_semaphore()
    if everyone:
        for d in range(1, n):
            pl.semaphore_signal(
                barrier, inc=1, device_id={"fsdp": lax.rem(me + d, n)}, device_id_type=MESH
            )
        pl.semaphore_wait(barrier, n - 1)
        return
    core = lax.rem(me, 2)
    pl.semaphore_signal(
        barrier, inc=1, device_id={"fsdp": me + 1 - 2 * core}, device_id_type=MESH
    )
    for d in range(1, n // 2):
        pl.semaphore_signal(
            barrier, inc=1, device_id={"fsdp": lax.rem(me + 2 * d, n)}, device_id_type=MESH
        )
    pl.semaphore_wait(barrier, n // 2)


def exchange_kernel(n, n_gather, n_swap, *refs):
    k = n_gather + n_swap
    ins, outs, sems = refs[:k], refs[k : 2 * k], refs[2 * k :]
    me = lax.axis_index("fsdp")
    core = lax.rem(me, 2)
    partner = me + 1 - 2 * core
    peer_barrier(n, me, n_swap > 0)
    pending, arrivals = [], []
    for a in range(n_gather):
        x, o = ins[a], outs[a]
        rows = x.shape[0]
        send, recv, fsend, frecv, local = sems[5 * a : 5 * a + 5]

        def block(i, o=o, rows=rows):
            return o.at[pl.ds(pl.multiple_of(i * rows, rows), rows)]

        for d in range(1, n // 2):
            copy = pltpu.make_async_remote_copy(
                x, block(me), send.at[d], recv.at[d],
                device_id={"fsdp": lax.rem(me + 2 * d, n)}, device_id_type=MESH,
            )
            copy.start()
            arrivals.append((copy, block(lax.rem(me + n - 2 * d, n)), fsend.at[d], frecv.at[d]))
        copy = pltpu.make_async_remote_copy(
            x, block(me), fsend.at[0], frecv.at[0],
            device_id={"fsdp": partner}, device_id_type=MESH,
        )
        copy.start()
        pending.append(copy)
        own = pltpu.make_async_copy(x, block(me), local.at[0])
        own.start()
        pending.append(own)
    for b in range(n_swap):
        x, o = ins[n_gather + b], outs[n_gather + b]
        send, recv, local = sems[5 * n_gather + 3 * b : 5 * n_gather + 3 * b + 3]
        for d in range(1, n):
            to = lax.rem(me + d, n)
            copy = pltpu.make_async_remote_copy(
                x.at[to], o.at[me], send.at[d], recv.at[d],
                device_id={"fsdp": to}, device_id_type=MESH,
            )
            copy.start()
            pending.append(copy)
        own = pltpu.make_async_copy(x.at[me], o.at[me], local.at[0])
        own.start()
        pending.append(own)
    for copy, landed, fs, fr in arrivals:
        copy.wait_recv()
        onward = pltpu.make_async_remote_copy(
            landed, landed, fs, fr, device_id={"fsdp": partner}, device_id_type=MESH
        )
        onward.start()
        pending.append(onward)
    for copy, _, _, _ in arrivals:
        copy.wait_send()
    for copy in pending:
        copy.wait()


def exchange(n, cid, gathers, swaps=()):
    k = len(gathers) + len(swaps)
    dma = pltpu.SemaphoreType.DMA
    sems = []
    for _ in gathers:
        sems += [dma((n // 2,)), dma((n // 2,)), dma((n // 2,)), dma((n // 2,)), dma((1,))]
    for _ in swaps:
        sems += [dma((n,)), dma((n,)), dma((1,))]
    shapes = [jax.ShapeDtypeStruct((n * g.shape[0],) + g.shape[1:], g.dtype) for g in gathers]
    shapes += [jax.ShapeDtypeStruct(s.shape, s.dtype) for s in swaps]
    return pl.pallas_call(
        functools.partial(exchange_kernel, n, len(gathers), len(swaps)),
        out_shape=tuple(shapes),
        in_specs=[pl.BlockSpec(memory_space=pl.ANY)] * k,
        out_specs=tuple([pl.BlockSpec(memory_space=pl.ANY)] * k),
        scratch_shapes=sems,
        compiler_params=pltpu.CompilerParams(collective_id=cid, has_side_effects=True),
        name=f"exchange{cid}",
    )(*gathers, *swaps)


def scatter_kernel(n, p_ref, o_ref, mine, theirs, sums, came, lsem, psend, precv, send, recv):
    me = lax.axis_index("fsdp")
    core = lax.rem(me, 2)
    partner = me + 1 - 2 * core
    chips = n // 2
    chip = (me - core) // 2
    rows = o_ref.shape[0]
    peer_barrier(n, me, False)

    def block(i):
        return p_ref.at[pl.ds(pl.multiple_of(i * rows, rows), rows)]

    order = list(range(1, chips)) + [0]
    pairs = {}
    for d in order:
        to = lax.rem(chip + d, chips)
        give = pltpu.make_async_remote_copy(
            block(2 * to + 1 - core), theirs.at[d], psend.at[d], precv.at[d],
            device_id={"fsdp": partner}, device_id_type=MESH,
        )
        give.start()
        keep = pltpu.make_async_copy(block(2 * to + core), mine.at[d], lsem.at[d])
        keep.start()
        pairs[d] = (give, keep)
    sent = []
    for d in order:
        give, keep = pairs[d]
        keep.wait()
        give.wait_recv()
        if d:
            sums[d] = (mine[d].astype(F32) + theirs[d].astype(F32)).astype(BF)
            copy = pltpu.make_async_remote_copy(
                sums.at[d], came.at[d], send.at[d], recv.at[d],
                device_id={"fsdp": lax.rem(me + 2 * d, n)}, device_id_type=MESH,
            )
            copy.start()
            sent.append((d, copy))
        else:
            o_ref[...] = mine[0].astype(F32) + theirs[0].astype(F32)
    for d, copy in sent:
        copy.wait_recv()
        o_ref[...] += came[d].astype(F32)
    for _, copy in sent:
        copy.wait_send()
    for d in order:
        pairs[d][0].wait_send()


def scatter_sum(n, cid, partial):
    rows, cols = partial.shape[0] // n, partial.shape[1]
    chips = n // 2
    dma = pltpu.SemaphoreType.DMA
    buf = pltpu.VMEM((chips, rows, cols), BF)
    return pl.pallas_call(
        functools.partial(scatter_kernel, n),
        out_shape=jax.ShapeDtypeStruct((rows, cols), F32),
        in_specs=[pl.BlockSpec(memory_space=pl.ANY)],
        out_specs=pl.BlockSpec(memory_space=pltpu.VMEM),
        scratch_shapes=[buf, buf, buf, buf] + [dma((chips,))] * 5,
        compiler_params=pltpu.CompilerParams(collective_id=cid, has_side_effects=True),
        name=f"scatter{cid}",
    )(partial)


def lane_heads(shape, size):
    return lax.broadcasted_iota(jnp.int32, shape, 1) // size


def dot_nt(a, b):
    return lax.dot_general(a, b, (((1,), (1,)), ((), ())), preferred_element_type=F32)


def attn_fwd_kernel(nh, hs, bk, z_ref, q_ref, kv_ref, o_ref, lse_ref):
    bq, w = q_ref.shape
    start = z_ref[0] * (bq * pl.num_programs(0)) + pl.program_id(0) * bq
    heads = lane_heads((bq, w), hs)
    q = q_ref[...]
    qh = [jnp.where(heads == h, q, jnp.zeros_like(q)) for h in range(nh)]

    def step(j, carry, masked):
        rows = pl.ds(pl.multiple_of(j * bk, bk), bk)
        k = kv_ref[rows, :w]
        v = kv_ref[rows, w:]
        out = []
        for h in range(nh):
            acc, tot = carry[h]
            e = jnp.exp(dot_nt(qh[h], k))
            if masked:
                qp = start + lax.broadcasted_iota(jnp.int32, e.shape, 0)
                kp = j * bk + lax.broadcasted_iota(jnp.int32, e.shape, 1)
                e = jnp.where(kp <= qp, e, 0.0)
            tot = tot + jnp.sum(e, axis=1, keepdims=True)
            acc = acc + jnp.dot(e.astype(BF), v, preferred_element_type=F32)
            out.append((acc, tot))
        return tuple(out)

    init = tuple((jnp.zeros((bq, w), F32), jnp.zeros((bq, 1), F32)) for _ in range(nh))
    full = start // bk
    last = (start + bq + bk - 1) // bk
    carry = lax.fori_loop(0, full, lambda j, c: step(j, c, False), init)
    carry = lax.fori_loop(full, last, lambda j, c: step(j, c, True), carry)
    out = carry[0][0] / carry[0][1]
    lse = jnp.broadcast_to(jnp.log(carry[0][1]), (bq, w))
    for h in range(1, nh):
        out = jnp.where(heads == h, carry[h][0] / carry[h][1], out)
        lse = jnp.where(heads == h, jnp.log(carry[h][1]), lse)
    o_ref[...] = out.astype(BF)
    lse_ref[...] = lse


def attn_dq_kernel(nh, hs, bk, scale, z_ref, q_ref, do_ref, o_ref, lse_ref, kv_ref, dq_ref):
    bq, w = q_ref.shape
    start = z_ref[0] * (bq * pl.num_programs(0)) + pl.program_id(0) * bq
    heads = lane_heads((bq, w), hs)
    q = q_ref[...]
    do = do_ref[...]
    prod = do.astype(F32) * o_ref[...].astype(F32)
    qh = [jnp.where(heads == h, q, jnp.zeros_like(q)) for h in range(nh)]
    dh = [jnp.where(heads == h, do, jnp.zeros_like(do)) for h in range(nh)]
    lse = [
        jnp.max(jnp.where(heads == h, lse_ref[...], -jnp.inf), axis=1, keepdims=True)
        for h in range(nh)
    ]
    delta = [
        jnp.sum(jnp.where(heads == h, prod, 0.0), axis=1, keepdims=True) for h in range(nh)
    ]

    def step(j, carry, masked):
        rows = pl.ds(pl.multiple_of(j * bk, bk), bk)
        k = kv_ref[rows, :w]
        v = kv_ref[rows, w:]
        out = []
        for h in range(nh):
            p = jnp.exp(dot_nt(qh[h], k) - lse[h])
            if masked:
                qp = start + lax.broadcasted_iota(jnp.int32, p.shape, 0)
                kp = j * bk + lax.broadcasted_iota(jnp.int32, p.shape, 1)
                p = jnp.where(kp <= qp, p, 0.0)
            ds = (p * (dot_nt(dh[h], v) - delta[h])).astype(BF)
            out.append(carry[h] + jnp.dot(ds, k, preferred_element_type=F32))
        return tuple(out)

    init = tuple(jnp.zeros((bq, w), F32) for _ in range(nh))
    full = start // bk
    last = (start + bq + bk - 1) // bk
    carry = lax.fori_loop(0, full, lambda j, c: step(j, c, False), init)
    carry = lax.fori_loop(full, last, lambda j, c: step(j, c, True), carry)
    out = carry[0]
    for h in range(1, nh):
        out = jnp.where(heads == h, carry[h], out)
    dq_ref[...] = (out * scale).astype(BF)


def attn_dkv_kernel(nh, hs, bq, z_ref, kv_ref, q_ref, do_ref, lse_ref, delta_ref, dkv_ref):
    bk = kv_ref.shape[0]
    w = q_ref.shape[1]
    total = q_ref.shape[0]
    start = z_ref[0] * (bk * pl.num_programs(0)) + pl.program_id(0) * bk
    heads = lane_heads((bk, w), hs)
    k = kv_ref[:, :w]
    v = kv_ref[:, w:]
    kh = [jnp.where(heads == h, k, jnp.zeros_like(k)) for h in range(nh)]
    vh = [jnp.where(heads == h, v, jnp.zeros_like(v)) for h in range(nh)]

    def step(i, carry, masked):
        rows = pl.ds(pl.multiple_of(i * bq, bq), bq)
        q = q_ref[rows, :]
        do = do_ref[rows, :]
        lse = lse_ref[:, rows]
        delta = delta_ref[:, rows]
        out = []
        for h in range(nh):
            dk, dv = carry[h]
            p = jnp.exp(dot_nt(kh[h], q) - lse[h : h + 1])
            if masked:
                kp = start + lax.broadcasted_iota(jnp.int32, p.shape, 0)
                qp = i * bq + lax.broadcasted_iota(jnp.int32, p.shape, 1)
                p = jnp.where(kp <= qp, p, 0.0)
            dv = dv + jnp.dot(p.astype(BF), do, preferred_element_type=F32)
            ds = (p * (dot_nt(vh[h], do) - delta[h : h + 1])).astype(BF)
            dk = dk + jnp.dot(ds, q, preferred_element_type=F32)
            out.append((dk, dv))
        return tuple(out)

    init = tuple((jnp.zeros((bk, w), F32), jnp.zeros((bk, w), F32)) for _ in range(nh))
    first = start // bq
    clear = (start + bk + bq - 1) // bq
    carry = lax.fori_loop(first, clear, lambda i, c: step(i, c, True), init)
    carry = lax.fori_loop(clear, total // bq, lambda i, c: step(i, c, False), carry)
    dk, dv = carry[0]
    for h in range(1, nh):
        dk = jnp.where(heads == h, carry[h][0], dk)
        dv = jnp.where(heads == h, carry[h][1], dv)
    dkv_ref[:, :w] = dk.astype(BF)
    dkv_ref[:, w:] = dv.astype(BF)


def gridded(kernel, steps, blocks, wholes, outs, args):
    vm = pltpu.VMEM

    def cut(shape):
        return pl.BlockSpec((shape[0] // steps, shape[1]), lambda i, z: (i, 0), memory_space=vm)

    def whole(shape):
        return pl.BlockSpec(shape, lambda i, z: (0, 0), memory_space=vm)

    specs = [cut(a.shape) for a in blocks] + [whole(a.shape) for a in wholes]
    many = isinstance(outs, tuple)
    return pl.pallas_call(
        kernel,
        out_shape=outs,
        grid_spec=pltpu.PrefetchScalarGridSpec(
            num_scalar_prefetch=1,
            grid=(steps,),
            in_specs=specs,
            out_specs=tuple(cut(o.shape) for o in outs) if many else cut(outs.shape),
        ),
        compiler_params=pltpu.CompilerParams(vmem_limit_bytes=56 * 2**20),
    )(args, *blocks, *wholes)


def on_device(
    block_input, out_grad, attn_gain, attn_shift, qkv_weight, query_bias, value_bias,
    out_weight, out_bias, mlp_gain, mlp_shift, fc_weight, fc_bias, proj_weight, proj_bias,
):
    tok, width = block_input.shape
    n = lax.axis_size("fsdp")
    me = lax.axis_index("fsdp")
    z_arr = lax.axis_index("seq").astype(jnp.int32).reshape(1)
    hs = width // HEADS
    w = width // n
    nh = w // hs
    scale = 1.0 / math.sqrt(hs)
    piece = n * tok
    bq = 512

    vecs = jnp.stack([attn_gain, attn_shift, out_bias, mlp_gain, mlp_shift, proj_bias])
    vecs = jnp.pad(vecs, ((0, 10), (0, 0)))
    w_cut = jnp.transpose(qkv_weight.reshape(w, 3, n, w), (2, 0, 1, 3)).reshape(n, w, 3 * w)
    x_all, vec_all, w_mine = exchange(n, 1, (block_input, vecs), (w_cut,))
    g_all = lax.all_gather(out_grad, "fsdp", axis=0, tiled=True)
    w_mine = w_mine.reshape(width, 3 * w)
    full = jnp.transpose(vec_all.reshape(n, 16, w), (1, 0, 2)).reshape(16, width).astype(F32)
    gain1, shift1, out_b, gain2, shift2, proj_b = (full[i] for i in range(6))

    normed_all, _ = norm_stats(x_all.astype(F32))
    norm1 = (normed_all * gain1 + shift1).astype(BF)
    qkv = jnp.dot(norm1, w_mine, preferred_element_type=F32)
    q = (qkv[:, :w] + query_bias.astype(F32)).astype(BF) * jnp.asarray(scale, BF)
    bias_kv = jnp.concatenate([jnp.zeros((w,), F32), value_bias.astype(F32)])
    kv = (qkv[:, w:] + bias_kv).astype(BF)
    kv_all = lax.all_gather(kv, "seq", axis=0, tiled=True)
    q_all = lax.all_gather(q, "seq", axis=0, tiled=True)

    bf_w = jax.ShapeDtypeStruct((piece, w), BF)
    attn, lse = gridded(
        functools.partial(attn_fwd_kernel, nh, hs, bq), piece // bq, (q,), (kv_all,),
        (bf_w, jax.ShapeDtypeStruct((piece, w), F32)), z_arr,
    )
    o_all = lax.all_gather(attn, "seq", axis=0, tiled=True)
    lse_all = lax.all_gather(lse[:, ::hs].T, "seq", axis=1, tiled=True)

    part = jnp.dot(attn, out_weight, preferred_element_type=F32).astype(BF)
    x_vals = block_input.astype(F32)
    resid1 = x_vals + scatter_sum(n, 2, part) + out_b
    normed2, rstd2 = norm_stats(resid1)
    norm2 = (normed2 * gain2 + shift2).astype(BF)
    (norm2_all,) = exchange(n, 3, (norm2,))

    pre = jnp.dot(norm2_all, fc_weight, preferred_element_type=F32) + fc_bias.astype(F32)
    tanh_val = jnp.tanh(gelu_coef * (pre + cubic_coef * pre * pre * pre))
    hidden = (0.5 * pre * (1.0 + tanh_val)).astype(BF)
    slope = 0.5 * (1.0 + tanh_val) + 0.5 * pre * (1.0 - tanh_val * tanh_val) * gelu_coef * (
        1.0 + 3.0 * cubic_coef * pre * pre
    )
    hidden_grad = jnp.einsum("td,fd->tf", g_all, proj_weight, preferred_element_type=F32)
    pre_grad = (hidden_grad * slope).astype(BF)
    part = jnp.einsum("tf,df->td", pre_grad, fc_weight, preferred_element_type=F32).astype(BF)
    norm2_grad = scatter_sum(n, 4, part)

    grad_vals = out_grad.astype(F32)
    resid1_grad = grad_vals + norm_backward(norm2_grad, normed2, rstd2, gain2)
    (r_all,) = exchange(n, 5, (resid1_grad.astype(BF),))

    attn_grad = jnp.einsum("te,de->td", r_all, out_weight, preferred_element_type=F32).astype(BF)
    do_all = lax.all_gather(attn_grad, "seq", axis=0, tiled=True)
    dq = gridded(
        functools.partial(attn_dq_kernel, nh, hs, bq, scale), piece // bq,
        (q, attn_grad, attn, lse), (kv_all,), bf_w, z_arr,
    )

    mlp_part = jnp.dot(hidden, proj_weight, preferred_element_type=F32).astype(BF)
    g_proj = jnp.einsum("tf,td->fd", hidden, g_all, preferred_element_type=F32)
    g_fc = jnp.einsum("td,tf->df", norm2_all, pre_grad, preferred_element_type=F32)
    g_out = jnp.einsum("td,te->de", attn, r_all, preferred_element_type=F32)
    t_proj = lax.psum(g_proj.astype(BF), "seq").astype(F32)
    t_fc = lax.psum(g_fc.astype(BF), "seq").astype(F32)
    t_out = lax.psum(g_out.astype(BF), "seq").astype(F32)
    block_output = (resid1 + scatter_sum(n, 6, mlp_part) + proj_b).astype(BF)

    prod = do_all.astype(F32) * o_all.astype(F32)
    lane = jnp.arange(w) // hs
    delta_all = jnp.stack(
        [jnp.sum(jnp.where(lane == h, prod, 0.0), axis=1) for h in range(nh)]
    )
    dkv = gridded(
        functools.partial(attn_dkv_kernel, nh, hs, bq), piece // bq, (kv,),
        (q_all, do_all, lse_all, delta_all), jax.ShapeDtypeStruct((piece, 2 * w), BF), z_arr,
    )
    d_all = jnp.concatenate([dq, dkv], axis=1)
    part = jnp.einsum("tc,dc->td", d_all, w_mine, preferred_element_type=F32).astype(BF)
    norm1_grad = scatter_sum(n, 7, part)
    g_qkv = jnp.einsum("td,tc->dc", norm1, d_all, preferred_element_type=F32).astype(BF)
    (g_back,) = exchange(n, 8, (), (g_qkv.reshape(n, w, 3 * w),))
    g_back = lax.psum(g_back, "seq").astype(F32)
    t_qkv = jnp.transpose(g_back.reshape(n, w, 3, w), (1, 2, 0, 3)).reshape(w, 3 * width)

    normed1, rstd1 = norm_stats(x_vals)
    input_grad = resid1_grad + norm_backward(norm1_grad, normed1, rstd1, gain1)

    ff = fc_bias.shape[0] * n

    def slot(vec, size):
        return lax.dynamic_update_slice_in_dim(
            jnp.zeros((size,), F32), vec, me * vec.shape[0], 0
        )

    sums = [
        jnp.sum(norm1_grad * normed1, axis=0),
        jnp.sum(norm1_grad, axis=0),
        slot(jnp.sum(dq.astype(F32), axis=0), width),
        slot(jnp.sum(dkv[:, w:].astype(F32), axis=0), width),
        jnp.sum(resid1_grad, axis=0),
        jnp.sum(norm2_grad * normed2, axis=0),
        jnp.sum(norm2_grad, axis=0),
        slot(jnp.sum(pre_grad.astype(F32), axis=0), ff),
        jnp.sum(grad_vals, axis=0),
    ]
    joined = lax.psum(jnp.concatenate(sums), ("seq", "fsdp"))
    vec_out, at = [], 0
    for s in sums:
        size = s.shape[0]
        vec_out.append(lax.dynamic_slice_in_dim(joined, at + me * (size // n), size // n, 0))
        at += size
    a_gain, a_shift, q_b, v_b, o_b, m_gain, m_shift, f_b, p_b = vec_out
    return (
        block_output, input_grad, a_gain, a_shift, t_qkv, q_b, v_b, t_out, o_b,
        m_gain, m_shift, t_fc, f_b, t_proj, p_b,
    )


def solution(mesh):
    rows, vec, row, col = P(("seq", "fsdp"), None), P("fsdp"), P("fsdp", None), P(None, "fsdp")
    params = (vec, vec, row, vec, vec, row, vec, vec, vec, col, vec, row, vec)
    return jax.shard_map(
        on_device,
        mesh=mesh,
        in_specs=(rows, rows) + params,
        out_specs=(rows, rows) + params,
        check_vma=False,
    )
```

time: 736 us -> 460 us (0.62); the launches traced: 727 us -> 459 us
  Pallas kernels: 0 us -> 185 us
  waiting for transfers between devices: 268 us -> 119 us
  blocking collectives: 197 us -> 62.4 us
  matrix products: 157 us -> 35.4 us
  local copies, waits for them, and re-layouts: 56.9 us -> 17.5 us
    pallas_call x0 -> x11, Pallas kernels: none -> 185 us  [the longest x4 76.1 us: scatter_sum(): pl.pallas_call(functools.partial(scatter_kernel, n), out_shape=jax.ShapeD...]
    dot_general x66 -> x12, matrix products: 157 us -> 35.4 us  [the longest x1 4.64 us: on_device(): jnp.einsum('td,fd->tf', g_all, proj_weight, preferred_element_type=F32)]
    reduce_scatter x4 -> x0, waiting for transfers between devices: 93.1 us -> none  [the longest x1 65.2 us: on_device(): lax.psum_scatter(g_qkv.astype(jnp.bfloat16), 'fsdp', scatter_dimension=0,...]
    all_gather x11 -> x1, blocking collectives: 97.2 us -> 20 us  [on_device(): lse_all = lax.all_gather(lse[:, ::hs].T, 'seq', axis=1, tiled=True)]
    all_to_all x3 -> x0, blocking collectives: 62 us -> none  [the longest x1 24.9 us: on_device(): lax.all_to_all(qkv_bf.reshape(1, tok_local, 3, groups, group_width), 'seq...]
    all_gather x7 -> x5, waiting for transfers between devices: 113 us -> 66.5 us  [the longest x1 45.7 us: on_device(): kv_all = lax.all_gather(kv, 'seq', axis=0, tiled=True)]
    psum x1, blocking collectives: 12.7 us -> 42.4 us  [on_device(): joined = lax.psum(jnp.concatenate(sums), ('seq', 'fsdp'))]
    unnamed x1 -> x0, blocking collectives: 25.2 us -> none
  transfers between devices with their start and end apart: 13 -> 6, of which waited for: 7 -> 3; matrix products, arithmetic and copies ran while one was open for 31% -> 11% of each run, Pallas kernels for 0% -> 27%
where the time goes in v1:
time: 460 us; the launch traced here: 459 us
  Pallas kernels  185 us (40%)
  waiting for transfers between devices  119 us (26%)
  blocking collectives  62.4 us (14%)
  matrix products  35.4 us (8%)
  other arithmetic  24.7 us (5%)
  local copies, waits for them, and re-layouts  17.5 us (4%)
  between operations  14.7 us (3%)
    pallas_call x4, Pallas kernels, scatter_sum(): pl.pallas_call(functools.partial(scatter_kernel, n), out_shape=jax.ShapeD...  76.1 us
    pallas_call x4, Pallas kernels, exchange(): pl.pallas_call(functools.partial(exchange_kernel, n, len(gathers), len(sw...  71.4 us
    psum x1, waiting for transfers between devices, on_device(): g_back = lax.psum(g_back, 'seq').astype(F32)  50.7 us
    all_gather x1, waiting for transfers between devices, on_device(): kv_all = lax.all_gather(kv, 'seq', axis=0, tiled=True)  45.7 us
    psum x1, blocking collectives, on_device(): joined = lax.psum(jnp.concatenate(sums), ('seq', 'fsdp'))  42.4 us
    pallas_call x3, Pallas kernels, gridded(): pl.pallas_call(kernel, out_shape=outs, grid_spec=pltpu.PrefetchScalarGrid...  37.9 us
    all_gather x1, waiting for transfers between devices, on_device(): q_all = lax.all_gather(q, 'seq', axis=0, tiled=True)  20.8 us
    all_gather x1, blocking collectives, on_device(): lse_all = lax.all_gather(lse[:, ::hs].T, 'seq', axis=1, tiled=True)  20 us
  transfers between devices with their start and end apart: 6, of which 3 were waited for; matrix products, arithmetic and copies ran while one was open for 11% of the time, Pallas kernels for 27%

profile of v1, /device:TPU:0, one launch (start us, length us, event | category | flops | bytes accessed | tf_op | source)
XLA Modules:
  0.0 459.0 jit_solution(13678570095780876146)
XLA Ops:
  7.2 0.7 pad_convert_fusion
  8.0 1.5 copy.36
  9.7 1.2 copy.38.refs_2_
  10.9 0.6 pad.6.refs_1_
  11.5 25.1 %exchange1.1 = (bf16[1024,1024]{1,0:T(8,128)(2,1)}, bf16[128,128]{1,0:T(8,128)(2,1)}, bf16[8,128,384]{2,1,0:T(8,128)(2,1)}) custom-call(bf16[128,1024]{1,0:T(8,128)(2,1)} %refs_0_.1, bf16[16,128]{1,0:T(8,128)(2,1)} %pad.6.refs_1_, bf16[8,128,384]{2,1,0:T(8,128)(2,1)} %copy.38.refs_2_), custom_call_target="tpu_custom_call" | custom-call | tf_op jit(solution)/shard_map/exchange1/pallas_call | solution.py:126
  36.6 2.1 convert_reduce_fusion
  38.8 0.7 fusion.2
  39.6 0.8 fusion.5
  40.4 0.3 copy-done.27
  40.7 1.2 fusion.35
  42.0 0.9 fusion.13.kv_ref
  43.0 0.7 all-gather.8.cloned.1.call-update
  43.9 0.8 fusion.27.q_ref
  44.7 45.7 %all-gather.6.cloned.1.call-done.kv_ref = bf16[4096,256]{1,0:T(8,128)(2,1)} async-done(((bf16[1024,256]{1,0:T(8,128)(2,1)}), bf16[4096,256]{1,0:T(8,128)(2,1)}) %all-gather.6.cloned.1.call-update) | async-done | bytes 2097168 | tf_op jit(solution)/shard_map/all_gather | solution.py:388
  90.4 6.4 %shard_map.262 = (bf16[1024,128]{1,0:T(8,128)(2,1)}, f32[1024,128]{1,0:T(8,128)}) custom-call(s32[1]{0:T(128)} %bitcast.z_ref, bf16[1024,128]{1,0:T(8,128)(2,1)} %fusion.27.q_ref, bf16[4096,256]{1,0:T(8,128)(2,1)} %all-gather.6.cloned.1.call-done.kv_ref), custom_call_target="tpu_custom_call" | custom-call | tf_op jit(solution)/shard_map/pallas_call | solution.py:345
  97.0 3.0 convolution_convert_fusion.3.p_ref
  100.0 22.7 %scatter2.1 = f32[128,1024]{1,0:T(8,128)} custom-call(bf16[1024,1024]{1,0:T(8,128)(2,1)} %convolution_convert_fusion.3.p_ref), custom_call_target="tpu_custom_call" | custom-call | tf_op jit(solution)/shard_map/scatter2/pallas_call | solution.py:190
  122.7 1.3 fusion.31
  124.3 0.9 add_convert_fusion.1.refs_0_
  125.1 17.8 %exchange3.1 = bf16[1024,1024]{1,0:T(8,128)(2,1)} custom-call(bf16[128,1024]{1,0:T(8,128)(2,1)} %add_convert_fusion.1.refs_0_), custom_call_target="tpu_custom_call" | custom-call | tf_op jit(solution)/shard_map/exchange3/pallas_call | solution.py:126
  142.9 2.9 fusion.36
  145.8 1.3 copy-done.29
  147.1 2.8 convolution_convert_fusion.2.p_ref
  149.9 18.0 %scatter6.1 = f32[128,1024]{1,0:T(8,128)} custom-call(bf16[1024,1024]{1,0:T(8,128)(2,1)} %convolution_convert_fusion.2.p_ref), custom_call_target="tpu_custom_call" | custom-call | tf_op jit(solution)/shard_map/scatter6/pallas_call | solution.py:190
  167.9 4.6 %convert_reduce_fusion.1 = (f32[512]{0:T(512)S(1)}, bf16[1024,512]{1,0:T(8,128)(2,1)S(1)}) fusion(f32[1024,512]{1,0:T(8,128)} %copy-done.29, f32[512]{0:T(512)S(1)} %convert_element_type.115, bf16[1024,1024]{1,0:T(8,128)(2,1)} %all-gather.8.cloned.1.call-done, bf16[512,1024]{1,0:T(8,128)(2,1)S(1)} %copy-done), kind=kOutput, calls=%fused_computation.17 | convolution fusion | flops 1085275648 | bytes 6295552 | tf_op jit(solution)/shard_map/td,fd->tf/dot_general | solution.py:412
  172.6 1.0 copy-done.31
  173.5 2.6 convolution_convert_fusion.1.p_ref
  176.1 17.7 %scatter4.1 = f32[128,1024]{1,0:T(8,128)} custom-call(bf16[1024,1024]{1,0:T(8,128)(2,1)} %convolution_convert_fusion.1.p_ref), custom_call_target="tpu_custom_call" | custom-call | tf_op jit(solution)/shard_map/scatter4/pallas_call | solution.py:190
  193.8 1.3 multiply_reduce_fusion
  195.2 2.0 fusion.30
  197.2 0.8 copy-done.4
  198.0 0.7 convert_element_type.122.refs_0_
  198.7 16.8 %exchange5.1 = bf16[1024,1024]{1,0:T(8,128)(2,1)} custom-call(bf16[128,1024]{1,0:T(8,128)(2,1)} %convert_element_type.122.refs_0_), custom_call_target="tpu_custom_call" | custom-call | tf_op jit(solution)/shard_map/exchange5/pallas_call | solution.py:126
  215.5 3.2 convolution_convert_fusion.8.do_ref
  218.7 0.5 all-gather.10.cloned.1.call-update
  219.3 2.0 copy.39
  221.4 1.1 slice.44
  222.4 20.0 %all_gather.22.lse_ref = f32[2,4096]{1,0:T(2,128)} all-gather(f32[2,1024]{1,0:T(2,128)S(1)} %bitcast.64), channel_id=1, replica_groups=mesh['seq'=4,'fsdp'=8] {'seq'}, dimensions={1}, use_global_device_ids=true | all-gather | bytes 40960 | tf_op jit(solution)/shard_map/all_gather | solution.py:397
  242.4 2.1 convolution_convert_fusion.7
  244.5 7.1 %shard_map.263 = bf16[1024,128]{1,0:T(8,128)(2,1)} custom-call(s32[1]{0:T(128)} %bitcast.z_ref, bf16[1024,128]{1,0:T(8,128)(2,1)} %fusion.27.q_ref, bf16[1024,128]{1,0:T(8,128)(2,1)} %convolution_convert_fusion.8.do_ref, bf16[1024,128]{1,0:T(8,128)(2,1)} %get-tuple-element.23.o_ref, f32[1024,128]{1,0:T(8,128)} %get-tuple-element.24.lse_ref, ...), custom_call_target="tpu_custom_call" | custom-call | tf_op jit(solution)/shard_map/pallas_call | solution.py:345
  251.7 3.6 convolution_convert_fusion.5
  255.3 2.4 convolution_convert_fusion.4
  257.7 2.7 select_reduce_fusion.1
  260.4 0.6 pad_maximum_fusion.3.delta_ref
  261.0 20.8 %all-gather.10.cloned.1.call-done.q_ref = bf16[4096,128]{1,0:T(8,128)(2,1)} async-done(((bf16[1024,128]{1,0:T(8,128)(2,1)}), bf16[4096,128]{1,0:T(8,128)(2,1)}) %all-gather.10.cloned.1.call-update) | async-done | bytes 1048592 | tf_op jit(solution)/shard_map/all_gather | solution.py:389
  281.9 24.3 %shard_map.264 = bf16[1024,256]{1,0:T(8,128)(2,1)} custom-call(s32[1]{0:T(128)} %bitcast.z_ref, bf16[1024,256]{1,0:T(8,128)(2,1)} %fusion.13.kv_ref, bf16[4096,128]{1,0:T(8,128)(2,1)} %all-gather.10.cloned.1.call-done.q_ref, bf16[4096,128]{1,0:T(8,128)(2,1)} %all-gather.12.cloned.1.call-done.do_ref, f32[2,4096]{1,0:T(2,128)} %all_gather.22.lse_ref, ...), custom_call_target="tpu_custom_call" | custom-call | tf_op jit(solution)/shard_map/pallas_call | solution.py:345
  306.2 3.2 convolution_convert_fusion.6
  309.4 11.8 %exchange8.1 = bf16[8,128,384]{2,1,0:T(8,128)(2,1)} custom-call(bf16[8,128,384]{2,1,0:T(8,128)(2,1)} %bitcast.54), custom_call_target="tpu_custom_call" | custom-call | tf_op jit(solution)/shard_map/exchange8/pallas_call | solution.py:126
  321.2 1.5 copy.40
  322.7 0.9 copy.41
  323.7 0.3 dynamic_update_slice.11
  324.1 0.5 dynamic_update_slice.9
  324.7 3.7 convolution_convert_fusion.p_ref
  328.4 17.8 %scatter7.1 = f32[128,1024]{1,0:T(8,128)} custom-call(bf16[1024,1024]{1,0:T(8,128)(2,1)} %convolution_convert_fusion.p_ref), custom_call_target="tpu_custom_call" | custom-call | tf_op jit(solution)/shard_map/scatter7/pallas_call | solution.py:190
  346.6 1.3 fusion.23
  348.0 42.4 %psum.35 = f32[12288]{0:T(1024)S(1)} all-reduce(f32[12288]{0:T(1024)S(1)} %constant_dynamic-update-slice_fusion), channel_id=1, replica_groups=mesh['seq'=4,'fsdp'=8] {'seq','fsdp'}, use_global_device_ids=true, to_apply=%region_21.22 | all-reduce | flops 12288 | bytes 98304 | tf_op jit(solution)/shard_map/psum | solution.py:475
  390.4 0.7 dynamic_slice.34
  391.1 0.6 fusion.34
  391.7 2.1 fusion.22
  393.8 50.7 %all-reduce.5.cloned.1.call-done = (bf16[128,3072]{0,1:T(8,128)(2,1)}, bf16[128,1024]{1,0:T(8,128)(2,1)}, bf16[1024,512]{1,0:T(8,128)(2,1)}, bf16[512,1024]{1,0:T(8,128)(2,1)}) async-done(((bf16[128,3072]{0,1:T(8,128)(2,1)}, bf16[128,1024]{1,0:T(8,128)(2,1)}, bf16[1024,512]{1,0:T(8,128)(2,1)}, bf16[512,1024]{1,0:T(8,128)(2,1)}), (bf16[128,3072]{0,1:T(8,128)(2,1)}, bf16[128,1024]{1,0:T(8,128)(2,1)}, ...) | async-done | bytes 3145744 | tf_op jit(solution)/shard_map/psum | solution.py:451
  444.6 1.9 convert_element_type.132
  446.4 2.5 copy.42
  449.0 1.6 convert_element_type.134
  450.6 1.6 convert_element_type.136
  (106 shorter events, 1.9 us)
Async XLA Ops:
  7.2 139.9 %copy-start = (bf16[512,1024]{1,0:T(8,128)(2,1)S(1)}, bf16[512,1024]{1,0:T(8,128)(2,1)}, u32[]{:S(2)}) copy-start(bf16[512,1024]{1,0:T(8,128)(2,1)} %param.28) | copy-start | bytes 3145732
  7.2 83.2 %all-gather.6.cloned.1.call-start = ((), (), s32[]{:S(2)}) async-start(), calls=%async_computation | async-start | bytes 2621440 | tf_op jit(solution)/shard_map/all_gather | solution.py:388
  8.0 2.9 copy-start.19
  8.0 2.9 copy-start.20
  8.0 2.9 copy-start.21
  8.0 2.8 copy-start.22
  8.0 2.8 copy-start.23
  8.0 2.8 copy-start.24
  36.6 2.2 copy-start.2
  36.6 2.9 copy-start.17
  39.6 1.1 copy-start.27
  40.4 1.6 copy-start.7
  42.0 1.7 copy-start.28
  42.0 1.8 copy-start.18
  42.0 1.8 copy-start.3
  42.9 54.1 %copy-start.13 = (bf16[128,1024]{1,0:T(8,128)(2,1)S(1)}, bf16[128,1024]{1,0:T(8,128)(2,1)}, u32[]{:S(2)}) copy-start(bf16[128,1024]{1,0:T(8,128)(2,1)} %param.22) | copy-start | bytes 786436
  42.9 125.0 %all-gather.8.cloned.1.call-start = ((), (), s32[]{:S(2)}) async-start(), calls=%async_computation.1 | async-start | bytes 2359296 | tf_op jit(solution)/shard_map/all_gather | solution.py:377
  43.7 214.0 %all-gather.14.cloned.1.call-start = ((), (), s32[]{:S(2)}) async-start(), calls=%async_computation.4 | async-start | bytes 1310720 | tf_op jit(solution)/shard_map/all_gather | solution.py:396
  96.8 160.9 %all-gather.12.cloned.1.call-start = ((), (), s32[]{:S(2)}) async-start(), calls=%async_computation.3 | async-start | bytes 1310720 | tf_op jit(solution)/shard_map/all_gather | solution.py:422
  124.0 18.9 %copy-start.26 = (bf16[1024,512]{1,0:T(8,128)(2,1)S(1)}, bf16[1024,512]{1,0:T(8,128)(2,1)}, u32[]{:S(2)}) copy-start(bf16[1024,512]{1,0:T(8,128)(2,1)} %param.26) | copy-start | bytes 3145732
  145.8 1.3 copy-start.29
  172.6 1.0 copy-start.31
  176.1 19.0 %copy-start.9 = (f32[128,1024]{1,0:T(8,128)S(1)}, f32[128,1024]{1,0:T(8,128)}, u32[]{:S(2)}) copy-start(f32[128,1024]{1,0:T(8,128)} %scatter6.1) | copy-start | bytes 1572868
  176.1 19.0 %copy-start.14 = (bf16[128,1024]{1,0:T(8,128)(2,1)S(1)}, bf16[128,1024]{1,0:T(8,128)(2,1)}, u32[]{:S(2)}) copy-start(bf16[128,1024]{1,0:T(8,128)(2,1)} %param.16) | copy-start | bytes 786436
  197.2 0.8 copy-start.4
  215.5 26.9 %copy-start.1 = (bf16[1024,1024]{1,0:T(8,128)(2,1)S(1)}, bf16[1024,1024]{1,0:T(8,128)(2,1)}, u32[]{:S(2)}) copy-start(bf16[1024,1024]{1,0:T(8,128)(2,1)} %exchange5.1) | copy-start | bytes 6291460
  218.7 63.2 %all-gather.10.cloned.1.call-start = ((), (), s32[]{:S(2)}) async-start(), calls=%async_computation.2 | async-start | bytes 1310720 | tf_op jit(solution)/shard_map/all_gather | solution.py:389
  219.3 225.3 %all-reduce.5.cloned.1.call-start = ((), (), s32[]{:S(2)}) async-start(), calls=%async_computation.5 | async-start | bytes 6291456 | tf_op jit(solution)/shard_map/psum | solution.py:451
  244.5 7.1 %copy-start.6 = (bf16[1024,1024]{1,0:T(8,128)(2,1)S(1)}, bf16[1024,1024]{1,0:T(8,128)(2,1)}, u32[]{:S(2)}) copy-start(bf16[1024,1024]{1,0:T(8,128)(2,1)} %exchange3.1) | copy-start | bytes 6291460
  251.6 3.7 copy-start.25
  251.7 3.7 copy-start.30
  260.4 45.8 %copy-start.8 = (bf16[1024,1024]{1,0:T(8,128)(2,1)S(1)}, bf16[1024,1024]{1,0:T(8,128)(2,1)}, u32[]{:S(2)}) copy-start(bf16[1024,1024]{1,0:T(8,128)(2,1)} %copy-done.7) | copy-start | bytes 6291460
  281.9 24.3 %copy-start.15 = (bf16[1024,128]{1,0:T(8,128)(2,1)S(1)}, bf16[1024,128]{1,0:T(8,128)(2,1)}, u32[]{:S(2)}) copy-start(bf16[1024,128]{1,0:T(8,128)(2,1)} %shard_map.263) | copy-start | bytes 786436
  322.7 1.3 copy-start.16
  323.6 1.0 copy-start.10
  328.4 63.3 %copy-start.5 = (f32[128,1024]{1,0:T(8,128)S(1)}, f32[128,1024]{1,0:T(8,128)}, u32[]{:S(2)}) copy-start(f32[128,1024]{1,0:T(8,128)} %copy-done.4) | copy-start | bytes 1572868
  444.6 4.4 copy-start.12
  449.0 1.6 copy-start.11
Sparse Core Ops, SparseCore 0:
  43.0 47.2 all-gather.5
  92.3 31.7 all-gather.7
  125.6 32.2 all-gather.13
  218.8 34.1 all-gather.11
  254.4 27.4 all-gather.9
  323.8 120.7 all-reduce.4

commit v2 on v1

--- a/solution.py
+++ b/solution.py
@@ -34,7 +34,7 @@
     )
 
 
-def peer_barrier(n, me, everyone):
+def peer_barrier(n, me, everyone, g=1, mez=None):
     barrier = pltpu.get_barrier_semaphore()
     if everyone:
         for d in range(1, n):
@@ -51,7 +51,11 @@
         pl.semaphore_signal(
             barrier, inc=1, device_id={"fsdp": lax.rem(me + 2 * d, n)}, device_id_type=MESH
         )
-    pl.semaphore_wait(barrier, n // 2)
+    for d in range(1, g):
+        pl.semaphore_signal(
+            barrier, inc=1, device_id={"seq": lax.rem(mez + d, g)}, device_id_type=MESH
+        )
+    pl.semaphore_wait(barrier, n // 2 + g - 1)
 
 
 def exchange_kernel(n, n_gather, n_swap, *refs):
@@ -134,14 +138,13 @@
     )(*gathers, *swaps)
 
 
-def scatter_kernel(n, p_ref, o_ref, mine, theirs, sums, came, lsem, psend, precv, send, recv):
+def scatter_body(n, p_ref, o_ref, mine, theirs, sums, came, lsem, psend, precv, send, recv):
     me = lax.axis_index("fsdp")
     core = lax.rem(me, 2)
     partner = me + 1 - 2 * core
     chips = n // 2
     chip = (me - core) // 2
     rows = o_ref.shape[0]
-    peer_barrier(n, me, False)
 
     def block(i):
         return p_ref.at[pl.ds(pl.multiple_of(i * rows, rows), rows)]
@@ -182,6 +185,173 @@
         pairs[d][0].wait_send()
 
 
+def scatter_kernel(n, *refs):
+    peer_barrier(n, lax.axis_index("fsdp"), False)
+    scatter_body(n, *refs)
+
+
+def tail_kernel(n, g, p_ref, gq_ref, o_ref, s_ref, *scratch):
+    bufs, (zin, zlocal, zsend, zrecv) = scratch[:9], scratch[9:]
+    me, mez = lax.axis_index("fsdp"), lax.axis_index("seq")
+    peer_barrier(n, me, False, g, mez)
+    own = pltpu.make_async_copy(gq_ref.at[mez], zin.at[0], zlocal.at[0])
+    own.start()
+    copies = []
+    for d in range(1, g):
+        to = lax.rem(mez + d, g)
+        copy = pltpu.make_async_remote_copy(
+            gq_ref.at[to], zin.at[d], zsend.at[d], zrecv.at[d],
+            device_id={"seq": to}, device_id_type=MESH,
+        )
+        copy.start()
+        copies.append(copy)
+    scatter_body(n, p_ref, o_ref, *bufs)
+    own.wait()
+    for copy in copies:
+        copy.wait()
+    total = zin[0].astype(F32)
+    for d in range(1, g):
+        total = total + zin[d].astype(F32)
+    s_ref[...] = total.astype(BF)
+
+
+def tail_scatter(n, g, cid, partial, gq):
+    rows, cols = partial.shape[0] // n, partial.shape[1]
+    chips = n // 2
+    dma = pltpu.SemaphoreType.DMA
+    buf = pltpu.VMEM((chips, rows, cols), BF)
+    return pl.pallas_call(
+        functools.partial(tail_kernel, n, g),
+        out_shape=(
+            jax.ShapeDtypeStruct((rows, cols), F32), jax.ShapeDtypeStruct(gq.shape[1:], BF),
+        ),
+        in_specs=[pl.BlockSpec(memory_space=pl.ANY)] * 2,
+        out_specs=(pl.BlockSpec(memory_space=pltpu.VMEM),) * 2,
+        scratch_shapes=[buf, buf, buf, buf] + [dma((chips,))] * 5
+        + [pltpu.VMEM(gq.shape, BF), dma((1,)), dma((g,)), dma((g,))],
+        compiler_params=pltpu.CompilerParams(collective_id=cid, has_side_effects=True),
+        name=f"tail{cid}",
+    )(partial, gq)
+
+
+def spread_kernel(n, g, s_ref, v_ref, out, vsum, came, *sems):
+    vlocal, vsend, vrecv, slocal, ssend, srecv, fsend, frecv = sems
+    me, mez = lax.axis_index("fsdp"), lax.axis_index("seq")
+    barrier = pltpu.get_barrier_semaphore()
+    others = [(dz, df) for dz in range(g) for df in range(n) if dz or df]
+
+    def dev(dz, df):
+        return {"seq": lax.rem(mez + dz, g), "fsdp": lax.rem(me + df, n)}
+
+    for dz, df in others:
+        pl.semaphore_signal(barrier, inc=1, device_id=dev(dz, df), device_id_type=MESH)
+    pl.semaphore_wait(barrier, n * g - 1)
+    pending = []
+    for df in range(1, n):
+        to = lax.rem(me + df, n)
+        copy = pltpu.make_async_remote_copy(
+            s_ref.at[to], out.at[mez, me], ssend.at[df], srecv.at[df],
+            device_id={"fsdp": to}, device_id_type=MESH,
+        )
+        copy.start()
+        pending.append(copy)
+    own = pltpu.make_async_copy(s_ref.at[me], out.at[mez, me], slocal.at[0])
+    own.start()
+    vown = pltpu.make_async_copy(v_ref.at[me], came.at[0], vlocal.at[0])
+    vown.start()
+    vcopies = []
+    for dz, df in others:
+        i = dz * n + df
+        copy = pltpu.make_async_remote_copy(
+            v_ref.at[lax.rem(me + df, n)], came.at[i], vsend.at[i], vrecv.at[i],
+            device_id=dev(dz, df), device_id_type=MESH,
+        )
+        copy.start()
+        vcopies.append(copy)
+    onward = []
+    for df in range(n):
+        if df:
+            pending[df - 1].wait_recv()
+        else:
+            own.wait()
+        landed = out.at[mez, lax.rem(me + n - df, n)]
+        for dz in range(1, g):
+            i = dz * n + df
+            copy = pltpu.make_async_remote_copy(
+                landed, landed, fsend.at[i], frecv.at[i],
+                device_id={"seq": lax.rem(mez + dz, g)}, device_id_type=MESH,
+            )
+            copy.start()
+            onward.append(copy)
+    vown.wait()
+    for copy in vcopies:
+        copy.wait()
+    vsum[...] = jnp.sum(came[...], axis=0)
+    for copy in pending:
+        copy.wait_send()
+    for copy in onward:
+        copy.wait()
+
+
+def spread(n, g, cid, s, v):
+    dma = pltpu.SemaphoreType.DMA
+    return pl.pallas_call(
+        functools.partial(spread_kernel, n, g),
+        out_shape=(
+            jax.ShapeDtypeStruct((g,) + s.shape, BF), jax.ShapeDtypeStruct(v.shape[1:], F32),
+        ),
+        in_specs=[pl.BlockSpec(memory_space=pl.ANY)] * 2,
+        out_specs=(
+            pl.BlockSpec(memory_space=pl.ANY), pl.BlockSpec(memory_space=pltpu.VMEM),
+        ),
+        scratch_shapes=[
+            pltpu.VMEM((g * n,) + v.shape[1:], F32),
+            dma((1,)), dma((g * n,)), dma((g * n,)),
+            dma((1,)), dma((n,)), dma((n,)), dma((g * n,)), dma((g * n,)),
+        ],
+        compiler_params=pltpu.CompilerParams(collective_id=cid, has_side_effects=True),
+        name=f"spread{cid}",
+    )(s, v)
+
+
+def rows_kernel(g, x_ref, o_ref, local, send, recv):
+    mez = lax.axis_index("seq")
+    cols = x_ref.shape[1]
+    barrier = pltpu.get_barrier_semaphore()
+    for d in range(1, g):
+        pl.semaphore_signal(
+            barrier, inc=1, device_id={"seq": lax.rem(mez + d, g)}, device_id_type=MESH
+        )
+    pl.semaphore_wait(barrier, g - 1)
+    here = o_ref.at[:, pl.ds(pl.multiple_of(mez * cols, cols), cols)]
+    own = pltpu.make_async_copy(x_ref, here, local.at[0])
+    own.start()
+    copies = []
+    for d in range(1, g):
+        copy = pltpu.make_async_remote_copy(
+            x_ref, here, send.at[d], recv.at[d],
+            device_id={"seq": lax.rem(mez + d, g)}, device_id_type=MESH,
+        )
+        copy.start()
+        copies.append(copy)
+    own.wait()
+    for copy in copies:
+        copy.wait()
+
+
+def gather_rows(g, cid, x):
+    dma = pltpu.SemaphoreType.DMA
+    return pl.pallas_call(
+        functools.partial(rows_kernel, g),
+        out_shape=jax.ShapeDtypeStruct((x.shape[0], g * x.shape[1]), x.dtype),
+        in_specs=[pl.BlockSpec(memory_space=pl.ANY)],
+        out_specs=pl.BlockSpec(memory_space=pl.ANY),
+        scratch_shapes=[dma((1,)), dma((g,)), dma((g,))],
+        compiler_params=pltpu.CompilerParams(collective_id=cid, has_side_effects=True),
+        name=f"rows{cid}",
+    )(x)
+
+
 def scatter_sum(n, cid, partial):
     rows, cols = partial.shape[0] // n, partial.shape[1]
     chips = n // 2
@@ -287,7 +457,7 @@
     dq_ref[...] = (out * scale).astype(BF)
 
 
-def attn_dkv_kernel(nh, hs, bq, z_ref, kv_ref, q_ref, do_ref, lse_ref, delta_ref, dkv_ref):
+def attn_dkv_kernel(nh, hs, bq, z_ref, kv_ref, q_ref, do_ref, stat_ref, dkv_ref):
     bk = kv_ref.shape[0]
     w = q_ref.shape[1]
     total = q_ref.shape[0]
@@ -302,18 +472,17 @@
         rows = pl.ds(pl.multiple_of(i * bq, bq), bq)
         q = q_ref[rows, :]
         do = do_ref[rows, :]
-        lse = lse_ref[:, rows]
-        delta = delta_ref[:, rows]
+        stat = stat_ref[:, rows]
         out = []
         for h in range(nh):
             dk, dv = carry[h]
-            p = jnp.exp(dot_nt(kh[h], q) - lse[h : h + 1])
+            p = jnp.exp(dot_nt(kh[h], q) - stat[h : h + 1])
             if masked:
                 kp = start + lax.broadcasted_iota(jnp.int32, p.shape, 0)
                 qp = i * bq + lax.broadcasted_iota(jnp.int32, p.shape, 1)
                 p = jnp.where(kp <= qp, p, 0.0)
             dv = dv + jnp.dot(p.astype(BF), do, preferred_element_type=F32)
-            ds = (p * (dot_nt(vh[h], do) - delta[h : h + 1])).astype(BF)
+            ds = (p * (dot_nt(vh[h], do) - stat[nh + h : nh + h + 1])).astype(BF)
             dk = dk + jnp.dot(ds, q, preferred_element_type=F32)
             out.append((dk, dv))
         return tuple(out)
@@ -360,7 +529,7 @@
     out_weight, out_bias, mlp_gain, mlp_shift, fc_weight, fc_bias, proj_weight, proj_bias,
 ):
     tok, width = block_input.shape
-    n = lax.axis_size("fsdp")
+    n, g = lax.axis_size("fsdp"), lax.axis_size("seq")
     me = lax.axis_index("fsdp")
     z_arr = lax.axis_index("seq").astype(jnp.int32).reshape(1)
     hs = width // HEADS
@@ -393,8 +562,6 @@
         functools.partial(attn_fwd_kernel, nh, hs, bq), piece // bq, (q,), (kv_all,),
         (bf_w, jax.ShapeDtypeStruct((piece, w), F32)), z_arr,
     )
-    o_all = lax.all_gather(attn, "seq", axis=0, tiled=True)
-    lse_all = lax.all_gather(lse[:, ::hs].T, "seq", axis=1, tiled=True)
 
     part = jnp.dot(attn, out_weight, preferred_element_type=F32).astype(BF)
     x_vals = block_input.astype(F32)
@@ -420,6 +587,12 @@
 
     attn_grad = jnp.einsum("te,de->td", r_all, out_weight, preferred_element_type=F32).astype(BF)
     do_all = lax.all_gather(attn_grad, "seq", axis=0, tiled=True)
+    prod = attn_grad.astype(F32) * attn.astype(F32)
+    lane = jnp.arange(w)
+    stats = [jnp.sum(jnp.where(lane == h * hs, lse, 0.0), axis=1) for h in range(nh)]
+    stats += [jnp.sum(jnp.where(lane // hs == h, prod, 0.0), axis=1) for h in range(nh)]
+    stats += [jnp.zeros((piece,), F32)] * (-2 * nh % 8)
+    stat_all = gather_rows(g, 6, jnp.stack(stats))
     dq = gridded(
         functools.partial(attn_dq_kernel, nh, hs, bq, scale), piece // bq,
         (q, attn_grad, attn, lse), (kv_all,), bf_w, z_arr,
@@ -432,56 +605,48 @@
     t_proj = lax.psum(g_proj.astype(BF), "seq").astype(F32)
     t_fc = lax.psum(g_fc.astype(BF), "seq").astype(F32)
     t_out = lax.psum(g_out.astype(BF), "seq").astype(F32)
-    block_output = (resid1 + scatter_sum(n, 6, mlp_part) + proj_b).astype(BF)
-
-    prod = do_all.astype(F32) * o_all.astype(F32)
-    lane = jnp.arange(w) // hs
-    delta_all = jnp.stack(
-        [jnp.sum(jnp.where(lane == h, prod, 0.0), axis=1) for h in range(nh)]
-    )
+    mlp_out = lax.psum_scatter(mlp_part, "fsdp", scatter_dimension=0, tiled=True)
+    block_output = (resid1 + mlp_out.astype(F32) + proj_b).astype(BF)
+
     dkv = gridded(
         functools.partial(attn_dkv_kernel, nh, hs, bq), piece // bq, (kv,),
-        (q_all, do_all, lse_all, delta_all), jax.ShapeDtypeStruct((piece, 2 * w), BF), z_arr,
+        (q_all, do_all, stat_all), jax.ShapeDtypeStruct((piece, 2 * w), BF), z_arr,
     )
     d_all = jnp.concatenate([dq, dkv], axis=1)
     part = jnp.einsum("tc,dc->td", d_all, w_mine, preferred_element_type=F32).astype(BF)
-    norm1_grad = scatter_sum(n, 7, part)
     g_qkv = jnp.einsum("td,tc->dc", norm1, d_all, preferred_element_type=F32).astype(BF)
-    (g_back,) = exchange(n, 8, (), (g_qkv.reshape(n, w, 3 * w),))
-    g_back = lax.psum(g_back, "seq").astype(F32)
-    t_qkv = jnp.transpose(g_back.reshape(n, w, 3, w), (1, 2, 0, 3)).reshape(w, 3 * width)
+    g_qkv = jnp.transpose(g_qkv.reshape(n, g, w // g, 3 * w), (1, 0, 2, 3))
+    norm1_grad, g_part = tail_scatter(n, g, 7, part, g_qkv)
 
     normed1, rstd1 = norm_stats(x_vals)
     input_grad = resid1_grad + norm_backward(norm1_grad, normed1, rstd1, gain1)
 
-    ff = fc_bias.shape[0] * n
-
-    def slot(vec, size):
-        return lax.dynamic_update_slice_in_dim(
-            jnp.zeros((size,), F32), vec, me * vec.shape[0], 0
-        )
-
-    sums = [
+    whole = jnp.stack([
         jnp.sum(norm1_grad * normed1, axis=0),
         jnp.sum(norm1_grad, axis=0),
-        slot(jnp.sum(dq.astype(F32), axis=0), width),
-        slot(jnp.sum(dkv[:, w:].astype(F32), axis=0), width),
         jnp.sum(resid1_grad, axis=0),
         jnp.sum(norm2_grad * normed2, axis=0),
         jnp.sum(norm2_grad, axis=0),
-        slot(jnp.sum(pre_grad.astype(F32), axis=0), ff),
         jnp.sum(grad_vals, axis=0),
-    ]
-    joined = lax.psum(jnp.concatenate(sums), ("seq", "fsdp"))
-    vec_out, at = [], 0
-    for s in sums:
-        size = s.shape[0]
-        vec_out.append(lax.dynamic_slice_in_dim(joined, at + me * (size // n), size // n, 0))
-        at += size
-    a_gain, a_shift, q_b, v_b, o_b, m_gain, m_shift, f_b, p_b = vec_out
+    ])
+    own = jnp.concatenate([
+        jnp.sum(dq.astype(F32), axis=0),
+        jnp.sum(dkv[:, w:].astype(F32), axis=0),
+        jnp.sum(pre_grad.astype(F32), axis=0),
+    ]).reshape(-1, w)
+    here = (jnp.arange(n) == me)[:, None, None]
+    vec = jnp.concatenate(
+        [jnp.transpose(whole.reshape(-1, n, w), (1, 0, 2)), jnp.where(here, own[None], 0.0)],
+        axis=1,
+    )
+    vec = jnp.pad(vec, ((0, 0), (0, -vec.shape[1] % 8), (0, 0)))
+    g_back, v = spread(n, g, 8, g_part, vec)
+    t_qkv = jnp.transpose(g_back.reshape(g, n, w // g, 3, w), (0, 2, 3, 1, 4))
+    t_qkv = t_qkv.reshape(w, 3 * width).astype(F32)
+    f_b = v[8 : 6 + own.shape[0]].reshape(-1)
     return (
-        block_output, input_grad, a_gain, a_shift, t_qkv, q_b, v_b, t_out, o_b,
-        m_gain, m_shift, t_fc, f_b, t_proj, p_b,
+        block_output, input_grad, v[0], v[1], t_qkv, v[6], v[7], t_out, v[2],
+        v[3], v[4], t_fc, f_b, t_proj, v[5],
     )
 
 

time: 460 us -> 407 us (0.88)
  blocking collectives: 62.4 us -> 0 us
  Pallas kernels: 185 us -> 238 us
  waiting for transfers between devices: 119 us -> 79.7 us
    pallas_call x0 -> x3, Pallas kernels: none -> 99.5 us  [the longest x1 62.7 us: spread(): pl.pallas_call(functools.partial(spread_kernel, n, g), out_shape=(jax.Sha...]
    psum x1, waiting for transfers between devices: 50.7 us -> 0.76 us  [on_device(): t_out = lax.psum(g_out.astype(BF), 'seq').astype(F32)]
    psum x1 -> x0, blocking collectives: 42.4 us -> none  [on_device(): joined = lax.psum(jnp.concatenate(sums), ('seq', 'fsdp'))]
    pallas_call x4 -> x2, Pallas kernels: 76.1 us -> 40.3 us  [scatter_sum(): pl.pallas_call(functools.partial(scatter_kernel, n), out_shape=jax.ShapeD...]
    reduce_scatter x0 -> x1, waiting for transfers between devices: none -> 21.9 us  [on_device(): lax.psum_scatter(mlp_part, 'fsdp', scatter_dimension=0, tiled=True)]
    all_gather x1, waiting for transfers between devices: 20.8 us -> 0.02 us  [on_device(): q_all = lax.all_gather(q, 'seq', axis=0, tiled=True)]
    all_gather x1 -> x0, blocking collectives: 20 us -> none  [on_device(): lse_all = lax.all_gather(lse[:, ::hs].T, 'seq', axis=1, tiled=True)]
    pallas_call x4 -> x3, Pallas kernels: 71.4 us -> 59.9 us  [exchange(): pl.pallas_call(functools.partial(exchange_kernel, n, len(gathers), len(sw...]
  transfers between devices with their start and end apart: 6 -> 6, of which waited for: 3 -> 4; matrix products, arithmetic and copies ran while one was open for 11% -> 13% of each run, Pallas kernels for 27% -> 52%
where the time goes in v2:
time: 407 us; the launch traced here: 406 us
  Pallas kernels  238 us (58%)
  waiting for transfers between devices  79.7 us (20%)
  matrix products  33.2 us (8%)
  other arithmetic  23.6 us (6%)
  local copies, waits for them, and re-layouts  17 us (4%)
  between operations  14.6 us (4%)
    pallas_call x1, Pallas kernels, spread(): pl.pallas_call(functools.partial(spread_kernel, n, g), out_shape=(jax.Sha...  62.7 us
    pallas_call x3, Pallas kernels, exchange(): pl.pallas_call(functools.partial(exchange_kernel, n, len(gathers), len(sw...  59.9 us
    all_gather x1, waiting for transfers between devices, on_device(): kv_all = lax.all_gather(kv, 'seq', axis=0, tiled=True)  45.7 us
    pallas_call x2, Pallas kernels, scatter_sum(): pl.pallas_call(functools.partial(scatter_kernel, n), out_shape=jax.ShapeD...  40.3 us
    pallas_call x3, Pallas kernels, gridded(): pl.pallas_call(kernel, out_shape=outs, grid_spec=pltpu.PrefetchScalarGrid...  37.9 us
    pallas_call x1, Pallas kernels, tail_scatter(): pl.pallas_call(functools.partial(tail_kernel, n, g), out_shape=(jax.Shape...  29.4 us
    reduce_scatter x1, waiting for transfers between devices, on_device(): lax.psum_scatter(mlp_part, 'fsdp', scatter_dimension=0, tiled=True)  21.9 us
    all_gather x1, waiting for transfers between devices, on_device(): do_all = lax.all_gather(attn_grad, 'seq', axis=0, tiled=True)  9.99 us
  transfers between devices with their start and end apart: 6, of which 4 were waited for; matrix products, arithmetic and copies ran while one was open for 13% of the time, Pallas kernels for 52%

profile of v2, /device:TPU:0, one launch (start us, length us, event | category | flops | bytes accessed | tf_op | source)
XLA Modules:
  0.0 406.3 jit_solution(3973315833026473206)
XLA Ops:
  7.2 0.7 pad_convert_fusion
  8.0 1.5 copy.36
  9.7 1.2 copy.38.refs_2_
  10.9 0.6 pad.10.refs_1_
  11.5 25.1 %exchange1.1 = (bf16[1024,1024]{1,0:T(8,128)(2,1)}, bf16[128,128]{1,0:T(8,128)(2,1)}, bf16[8,128,384]{2,1,0:T(8,128)(2,1)}) custom-call(bf16[128,1024]{1,0:T(8,128)(2,1)} %refs_0_.1, bf16[16,128]{1,0:T(8,128)(2,1)} %pad.10.refs_1_, bf16[8,128,384]{2,1,0:T(8,128)(2,1)} %copy.38.refs_2_), custom_call_target="tpu_custom_call" | custom-call | tf_op jit(solution)/shard_map/exchange1/pallas_call | solution.py:130
  36.6 2.1 convert_reduce_fusion
  38.8 0.7 fusion.2
  39.6 0.8 fusion.5
  40.4 0.3 copy-done.29
  40.7 1.2 fusion.34
  42.0 0.9 fusion.13.kv_ref
  43.0 0.7 all-gather.7.cloned.1.call-update
  43.9 0.7 fusion.27.q_ref
  44.7 45.7 %all-gather.5.cloned.1.call-done.kv_ref = bf16[4096,256]{1,0:T(8,128)(2,1)} async-done(((bf16[1024,256]{1,0:T(8,128)(2,1)}), bf16[4096,256]{1,0:T(8,128)(2,1)}) %all-gather.5.cloned.1.call-update) | async-done | bytes 2097168 | tf_op jit(solution)/shard_map/all_gather | solution.py:557
  90.4 6.4 %shard_map.262 = (bf16[1024,128]{1,0:T(8,128)(2,1)}, f32[1024,128]{1,0:T(8,128)}) custom-call(s32[1]{0:T(128)} %bitcast.z_ref, bf16[1024,128]{1,0:T(8,128)(2,1)} %fusion.27.q_ref, bf16[4096,256]{1,0:T(8,128)(2,1)} %all-gather.5.cloned.1.call-done.kv_ref), custom_call_target="tpu_custom_call" | custom-call | tf_op jit(solution)/shard_map/pallas_call | solution.py:514
  96.8 3.0 convolution_convert_fusion.3.refs_0_
  99.7 22.4 %scatter2.1 = f32[128,1024]{1,0:T(8,128)} custom-call(bf16[1024,1024]{1,0:T(8,128)(2,1)} %convolution_convert_fusion.3.refs_0_), custom_call_target="tpu_custom_call" | custom-call | tf_op jit(solution)/shard_map/scatter2/pallas_call | solution.py:360
  122.2 1.3 fusion.31
  123.5 0.2 multiply_reduce_fusion.2
  123.7 0.9 add_convert_fusion.1.refs_0_
  124.6 18.1 %exchange3.1 = bf16[1024,1024]{1,0:T(8,128)(2,1)} custom-call(bf16[128,1024]{1,0:T(8,128)(2,1)} %add_convert_fusion.1.refs_0_), custom_call_target="tpu_custom_call" | custom-call | tf_op jit(solution)/shard_map/exchange3/pallas_call | solution.py:130
  142.6 2.8 fusion.35
  145.5 1.3 copy-done.32
  146.8 2.9 convolution_convert_fusion.2
  149.8 0.5 all-gather.9.cloned.1.call-update
  150.3 0.2 all-gather.11.cloned.1.call-start
  150.6 4.6 %convert_reduce_fusion.1 = (f32[512]{0:T(512)S(1)}, bf16[1024,512]{1,0:T(8,128)(2,1)S(1)}) fusion(f32[1024,512]{1,0:T(8,128)} %copy-done.32, f32[512]{0:T(512)S(1)} %convert_element_type.131, bf16[1024,1024]{1,0:T(8,128)(2,1)} %all-gather.7.cloned.1.call-done, bf16[512,1024]{1,0:T(8,128)(2,1)S(1)} %copy-done), kind=kOutput, calls=%fused_computation.17 | convolution fusion | flops 1085275648 | bytes 6295552 | tf_op jit(solution)/shard_map/td,fd->tf/dot_general | solution.py:579
  155.2 1.0 copy-done.34
  156.2 2.6 convolution_convert_fusion.1.refs_0_
  158.8 17.9 %scatter4.1 = f32[128,1024]{1,0:T(8,128)} custom-call(bf16[1024,1024]{1,0:T(8,128)(2,1)} %convolution_convert_fusion.1.refs_0_), custom_call_target="tpu_custom_call" | custom-call | tf_op jit(solution)/shard_map/scatter4/pallas_call | solution.py:360
  176.7 1.3 multiply_reduce_fusion
  178.1 21.9 %reduce-scatter.2.cloned.1.call-done = bf16[128,1024]{1,0:T(8,128)(2,1)} async-done(((bf16[1024,1024]{1,0:T(8,128)(2,1)}), bf16[128,1024]{1,0:T(8,128)(2,1)}) %reduce-scatter.2.cloned.1.call-update) | async-done | bytes 262160 | tf_op jit(solution)/shard_map/reduce_scatter | solution.py:608
  200.0 2.1 fusion.30
  202.1 0.8 copy-done.4
  202.9 0.7 convert_element_type.139.refs_0_
  203.6 16.8 %exchange5.1 = bf16[1024,1024]{1,0:T(8,128)(2,1)} custom-call(bf16[128,1024]{1,0:T(8,128)(2,1)} %convert_element_type.139.refs_0_), custom_call_target="tpu_custom_call" | custom-call | tf_op jit(solution)/shard_map/exchange5/pallas_call | solution.py:130
  220.4 3.1 select_reduce_fusion
  223.6 0.3 select_reduce_fusion.2
  224.0 4.3 %convolution_convert_fusion.5 = bf16[1024,512]{1,0:T(8,128)(2,1)} fusion(bf16[1024,1024]{1,0:T(8,128)(2,1)} %exchange3.1, bf16[1024,512]{1,0:T(8,128)(2,1)} %copy-done.34), kind=kOutput, calls=%fused_computation.24 | convolution fusion | flops 1074266112 | bytes 4194304 | tf_op jit(solution)/shard_map/td,tf->df/dot_general | solution.py:603
  228.3 2.4 convolution_convert_fusion.4
  230.7 0.7 stack.72.x_ref
  231.3 7.3 %rows6.1.stat_ref = f32[8,4096]{1,0:T(8,128)} custom-call(f32[8,1024]{1,0:T(8,128)} %stack.72.x_ref), custom_call_target="tpu_custom_call" | custom-call | tf_op jit(solution)/shard_map/rows6/pallas_call | solution.py:344
  238.7 7.3 %shard_map.263 = bf16[1024,128]{1,0:T(8,128)(2,1)} custom-call(s32[1]{0:T(128)} %bitcast.z_ref, bf16[1024,128]{1,0:T(8,128)(2,1)} %fusion.27.q_ref, bf16[1024,128]{1,0:T(8,128)(2,1)} %get-tuple-element.69.do_ref, bf16[1024,128]{1,0:T(8,128)(2,1)} %get-tuple-element.27.o_ref, f32[1024,128]{1,0:T(8,128)} %get-tuple-element.28.lse_ref, ...), custom_call_target="tpu_custom_call" | custom-call | tf_op jit(solution)/shard_map/pallas_call | solution.py:514
  245.9 1.1 convert_reduce_fusion.5
  247.0 1.2 convolution_convert_fusion.7
  248.3 10.0 %all-gather.11.cloned.1.call-done.do_ref = bf16[4096,128]{1,0:T(8,128)(2,1)} async-done(((bf16[1024,128]{1,0:T(8,128)(2,1)}), bf16[4096,128]{1,0:T(8,128)(2,1)}) %all-gather.11.cloned.1.call-update) | async-done | bytes 1048592 | tf_op jit(solution)/shard_map/all_gather | solution.py:589
  258.3 24.3 %shard_map.264 = bf16[1024,256]{1,0:T(8,128)(2,1)} custom-call(s32[1]{0:T(128)} %bitcast.z_ref, bf16[1024,256]{1,0:T(8,128)(2,1)} %fusion.13.kv_ref, bf16[4096,128]{1,0:T(8,128)(2,1)} %all-gather.9.cloned.1.call-done.q_ref, bf16[4096,128]{1,0:T(8,128)(2,1)} %all-gather.11.cloned.1.call-done.do_ref, f32[8,4096]{1,0:T(8,128)} %rows6.1.stat_ref), custom_call_target="tpu_custom_call" | custom-call | tf_op jit(solution)/shard_map/pallas_call | solution.py:514
  282.6 2.4 convolution_convert_fusion.6
  285.0 1.0 copy.44
  286.0 2.6 convolution_convert_fusion.p_ref
  288.6 29.4 %tail7.1 = (f32[128,1024]{1,0:T(8,128)}, bf16[8,32,384]{2,1,0:T(8,128)(2,1)}) custom-call(bf16[1024,1024]{1,0:T(8,128)(2,1)} %convolution_convert_fusion.p_ref, bf16[4,8,32,384]{3,2,1,0:T(8,128)(2,1)} %bitcast.85), custom_call_target="tpu_custom_call" | custom-call | tf_op jit(solution)/shard_map/tail7/pallas_call | solution.py:223
  318.0 1.3 fusion.23
  319.7 0.6 select_maximum_fusion.v_ref
  320.3 62.7 %spread8.1 = (bf16[4,8,32,384]{3,2,1,0:T(8,128)(2,1)}, f32[16,128]{1,0:T(8,128)}) custom-call(bf16[8,32,384]{2,1,0:T(8,128)(2,1)} %get-tuple-element.30.s_ref, f32[8,16,128]{2,1,0:T(8,128)} %select_maximum_fusion.v_ref), custom_call_target="tpu_custom_call" | custom-call | tf_op jit(solution)/shard_map/spread8/pallas_call | solution.py:298
  383.1 2.4 reshape.152
  385.5 2.1 copy.41
  387.5 2.6 reshape.150
  390.2 0.6 slice_bitcast_fusion
  390.8 0.5 slice_bitcast_fusion.1
  391.3 1.0 fusion.22
  392.4 0.8 all-reduce.6.cloned.1.call-done
  393.1 1.9 convert_element_type.153
  395.0 2.8 convert_element_type.155
  397.8 1.6 convert_element_type.157
  (101 shorter events, 1.2 us)
Async XLA Ops:
  7.2 139.6 %copy-start = (bf16[512,1024]{1,0:T(8,128)(2,1)S(1)}, bf16[512,1024]{1,0:T(8,128)(2,1)}, u32[]{:S(2)}) copy-start(bf16[512,1024]{1,0:T(8,128)(2,1)} %param.28) | copy-start | bytes 3145732
  7.2 83.2 %all-gather.5.cloned.1.call-start = ((), (), s32[]{:S(2)}) async-start(), calls=%async_computation.1 | async-start | bytes 2621440 | tf_op jit(solution)/shard_map/all_gather | solution.py:557
  8.0 2.9 copy-start.21
  8.0 2.9 copy-start.22
  8.0 2.9 copy-start.23
  8.0 2.8 copy-start.24
  8.0 2.8 copy-start.25
  8.0 2.8 copy-start.26
  36.6 2.2 copy-start.1
  36.6 2.9 copy-start.18
  39.6 1.1 copy-start.29
  40.4 1.6 copy-start.8
  42.0 1.7 copy-start.31
  42.0 1.7 copy-start.20
  42.0 1.8 copy-start.3
  42.9 53.9 %copy-start.17 = (bf16[128,1024]{1,0:T(8,128)(2,1)S(1)}, bf16[128,1024]{1,0:T(8,128)(2,1)}, u32[]{:S(2)}) copy-start(bf16[128,1024]{1,0:T(8,128)(2,1)} %param.22) | copy-start | bytes 786436
  42.9 107.7 %all-gather.7.cloned.1.call-start = ((), (), s32[]{:S(2)}) async-start(), calls=%async_computation.3 | async-start | bytes 2359296 | tf_op jit(solution)/shard_map/all_gather | solution.py:546
  43.7 156.3 %reduce-scatter.2.cloned.1.call-start = ((), (), s32[]{:S(2)}) async-start(), calls=%async_computation.2 | async-start | bytes 2359296 | tf_op jit(solution)/shard_map/reduce_scatter | solution.py:608
  123.5 19.2 %copy-start.28 = (bf16[1024,512]{1,0:T(8,128)(2,1)S(1)}, bf16[1024,512]{1,0:T(8,128)(2,1)}, u32[]{:S(2)}) copy-start(bf16[1024,512]{1,0:T(8,128)(2,1)} %param.26) | copy-start | bytes 3145732
  145.5 1.3 copy-start.32
  149.7 98.6 %all-gather.9.cloned.1.call-start = ((), (), s32[]{:S(2)}) async-start(), calls=%async_computation.4 | async-start | bytes 1310720 | tf_op jit(solution)/shard_map/all_gather | solution.py:558
  150.3 108.0 %all-gather.11.cloned.1.call-start = ((), (), s32[]{:S(2)}) async-start(), calls=%async_computation.5 | async-start | bytes 1310720 | tf_op jit(solution)/shard_map/all_gather | solution.py:589
  155.2 1.0 copy-start.34
  158.8 41.2 %copy-start.15 = (bf16[128,1024]{1,0:T(8,128)(2,1)S(1)}, bf16[128,1024]{1,0:T(8,128)(2,1)}, u32[]{:S(2)}) copy-start(bf16[128,1024]{1,0:T(8,128)(2,1)} %param.16) | copy-start | bytes 786436
  202.1 0.8 copy-start.4
  202.1 18.3 %copy-start.6 = (bf16[1024,128]{1,0:T(8,128)(2,1)S(1)}, bf16[1024,128]{1,0:T(8,128)(2,1)}, u32[]{:S(2)}) copy-start(bf16[1024,128]{1,0:T(8,128)(2,1)} %get-tuple-element.27.o_ref) | copy-start | bytes 786436
  220.4 3.2 copy-start.10
  223.6 169.6 %all-reduce.6.cloned.1.call-start = ((), (), s32[]{:S(2)}) async-start(), calls=%async_computation.6 | async-start | bytes 4718592 | tf_op jit(solution)/shard_map/psum | solution.py:607
  224.0 4.3 %copy-start.27 = (bf16[1024,1024]{1,0:T(8,128)(2,1)S(1)}, bf16[1024,1024]{1,0:T(8,128)(2,1)}, u32[]{:S(2)}) copy-start(bf16[1024,1024]{1,0:T(8,128)(2,1)} %all-gather.7.cloned.1.call-done) | copy-start | bytes 6291460
  224.0 4.3 %copy-start.33 = (f32[1024,512]{1,0:T(8,128)S(1)}, f32[1024,512]{1,0:T(8,128)}, u32[]{:S(2)}) copy-start(f32[1024,512]{1,0:T(8,128)} %copy-done.32) | copy-start | bytes 6291460
  230.7 16.4 %copy-start.2 = (bf16[1024,1024]{1,0:T(8,128)(2,1)S(1)}, bf16[1024,1024]{1,0:T(8,128)(2,1)}, u32[]{:S(2)}) copy-start(bf16[1024,1024]{1,0:T(8,128)(2,1)} %exchange5.1) | copy-start | bytes 6291460
  238.7 8.4 %copy-start.7 = (bf16[1024,128]{1,0:T(8,128)(2,1)S(1)}, bf16[1024,128]{1,0:T(8,128)(2,1)}, u32[]{:S(2)}) copy-start(bf16[1024,128]{1,0:T(8,128)(2,1)} %get-tuple-element.27.o_ref) | copy-start | bytes 786436
  248.3 34.3 %copy-start.9 = (bf16[1024,1024]{1,0:T(8,128)(2,1)S(1)}, bf16[1024,1024]{1,0:T(8,128)(2,1)}, u32[]{:S(2)}) copy-start(bf16[1024,1024]{1,0:T(8,128)(2,1)} %copy-done.8) | copy-start | bytes 6291460
  258.3 24.3 %copy-start.16 = (bf16[1024,128]{1,0:T(8,128)(2,1)S(1)}, bf16[1024,128]{1,0:T(8,128)(2,1)}, u32[]{:S(2)}) copy-start(bf16[1024,128]{1,0:T(8,128)(2,1)} %shard_map.263) | copy-start | bytes 786436
  282.6 3.4 copy-start.12
  282.6 3.4 copy-start.30
  288.6 30.8 %copy-start.13 = (bf16[1024,256]{1,0:T(8,128)(2,1)S(1)}, bf16[1024,256]{1,0:T(8,128)(2,1)}, u32[]{:S(2)}) copy-start(bf16[1024,256]{1,0:T(8,128)(2,1)} %shard_map.264) | copy-start | bytes 1572868
  387.5 2.6 copy-start.19
  387.5 3.8 copy-start.5
  387.5 3.8 copy-start.11
  393.1 4.7 %copy-start.14 = (bf16[512,1024]{1,0:T(8,128)(2,1)S(1)}, bf16[512,1024]{1,0:T(8,128)(2,1)}, u32[]{:S(2)}) copy-start(bf16[512,1024]{1,0:T(8,128)(2,1)} %get-tuple-element.47) | copy-start | bytes 3145732
Sparse Core Ops, SparseCore 0:
  43.0 47.2 all-gather.4
  92.3 31.4 all-gather.6
  149.8 50.1 reduce-scatter.1
  201.4 27.9 all-gather.8
  230.9 27.3 all-gather.10
  261.3 131.7 all-reduce.5
